TPU v7x, 32 devices: a whole 2x2x4 slice. The times are simulated.
32 devices in a mesh: ctx: 8 (over z, y), head: 4 (over x, core).
Axes of the slice: x: 2, y: 2, z: 4, core: 2. Of those that a mesh axis runs over, the one named last changes fastest.
Arguments:
- queries: bfloat16 [4096, 4096], P(('ctx', 'head')), may hold values from -6 to 6
- keys: bfloat16 [4096, 1024], P(('ctx', 'head')), may hold values from -6 to 6
- values: bfloat16 [4096, 1024], P(('ctx', 'head')), may hold values from -6 to 6
- cotangent: bfloat16 [4096, 4096], P(('ctx', 'head')), may hold values from -6 to 6
Outputs:
- out: bfloat16 [4096, 4096], P(('ctx', 'head'))
- grad_queries: bfloat16 [4096, 4096], P(('ctx', 'head'))
- grad_keys: bfloat16 [4096, 1024], P(('ctx', 'head'))
- grad_values: bfloat16 [4096, 1024], P(('ctx', 'head'))
All inputs are finite; a program needn't handle non-finite values.
Results may differ from a plain program's by a relative error of at most 0.008.
Values may be sent and summed in bfloat16 or wider, within the bound.
No kernel may reach another device: no remote copies, remote signals or barrier semaphores. Data moves between devices by JAX's collectives and lax.ppermute only.
A program may use at most 64 MiB of HBM per device.

v0:
```python
import jax
import jax.numpy as jnp
from jax import lax
from jax.experimental import pallas as pl
from jax.experimental.pallas import tpu as pltpu
from jax.sharding import PartitionSpec as P


QUERY_HEADS = 32
KEY_VALUE_HEADS = 8
DEPTH = 128
BLOCK = 512
TILE = 256
GROUP = QUERY_HEADS // KEY_VALUE_HEADS
LOWEST = -1e30
LOG2E = 1.4426950408889634

BF = jnp.bfloat16
F32 = jnp.float32


def dot(a, b, ca, cb):
    return lax.dot_general(a, b, (((ca,), (cb,)), ((), ())), preferred_element_type=F32)


VM = pl.BlockSpec(memory_space=pltpu.VMEM)
ROOM = pltpu.CompilerParams(vmem_limit_bytes=12 << 20)


def here(d):
    return lax.axis_index("head") ^ d


def rows_of(d, size):
    return pl.ds(pl.multiple_of(here(d) * size, size), size)


def pack_kv_kernel(k_ref, v_ref, *outs):
    sums_ref = outs[-1]
    blocks = sums_ref.shape[0]
    wide = 2 * DEPTH
    for d, out in enumerate(outs[:-1]):
        cols = rows_of(d, wide)
        out[:, :wide] = k_ref[:, cols]
        out[:, wide:] = v_ref[:, cols]
    for part in range(len(outs) - 1):
        cols = slice(part * wide, (part + 1) * wide)
        ks = jnp.sum(k_ref[:, cols].astype(F32), axis=0, keepdims=True)
        vs = jnp.sum(v_ref[:, cols].astype(F32), axis=0, keepdims=True)
        sums_ref[:, part, :wide] = jnp.broadcast_to(ks, (blocks, wide))
        sums_ref[:, part, wide:] = jnp.broadcast_to(vs, (blocks, wide))


def pack_kv(k, v, parts, blocks):
    rows = k.shape[0]
    outs = pl.pallas_call(
        pack_kv_kernel,
        out_shape=[jax.ShapeDtypeStruct((rows, 4 * DEPTH), BF)] * parts
        + [jax.ShapeDtypeStruct((blocks, parts, 4 * DEPTH), F32)],
        out_specs=[VM] * (parts + 1),
        compiler_params=ROOM, name="pack_kv",
    )(k, v)
    return outs[:-1], outs[-1]


def pack_kernel(*refs):
    parts = len(refs) // 3
    for d in range(parts):
        q_ref, g_ref, out = refs[d], refs[parts + d], refs[2 * parts + d]
        for i in range(GROUP):
            out[i, 0] = q_ref[:, i * DEPTH : (i + 1) * DEPTH]
            out[i, 1] = g_ref[:, i * DEPTH : (i + 1) * DEPTH]


def pack(q, g, which, parts):
    rows = q.shape[0]

    def spec(d):
        return pl.BlockSpec((rows, GROUP * DEPTH), lambda i: (0, 2 * here(d) + which))

    return pl.pallas_call(
        pack_kernel,
        grid=(1,),
        in_specs=[spec(d) for d in range(parts)] * 2,
        out_specs=[VM] * parts,
        out_shape=[jax.ShapeDtypeStruct((GROUP, 2, rows, DEPTH), BF)] * parts,
        compiler_params=ROOM, name="pack",
    )(*([q] * parts + [g] * parts))


def gather_kernel(*refs):
    a_ref, b_ref = refs[-2:]
    rows = refs[0].shape[0]
    for d, piece in enumerate(refs[:-2]):
        at = rows_of(d, rows)
        for which, out in enumerate((a_ref, b_ref)):
            out[at, :DEPTH] = piece[:, which * DEPTH : (which + 1) * DEPTH]
            out[at, DEPTH:] = piece[:, (2 + which) * DEPTH : (3 + which) * DEPTH]


def gather(pieces):
    return pl.pallas_call(
        gather_kernel,
        in_specs=[VM] * len(pieces),
        out_specs=[VM] * 2,
        out_shape=[jax.ShapeDtypeStruct((BLOCK, 2 * DEPTH), BF)] * 2,
        compiler_params=ROOM, name="gather_kv",
    )(*pieces)


def attend_kernel(parts, which, *refs):
    pieces = refs[:parts]
    kv_ref, prev_ref, sums_ref = refs[parts : parts + 3]
    outs = refs[parts + 3 : 2 * parts + 3]
    edge_ref, own_ref, ds_ref = refs[2 * parts + 3 : 2 * parts + 6]
    kc, vc, kt, vt, dk, dv, qs, gs, os, dqs = refs[2 * parts + 6 :]
    ctx = lax.axis_index("ctx")
    scale = DEPTH ** (-0.5)
    coef = scale * LOG2E
    count = sums_ref.shape[0]
    pad = kc.shape[0] - 2 * BLOCK
    small = BLOCK // parts

    mean = (jnp.sum(sums_ref[...], axis=1) * (1.0 / BLOCK)).astype(BF)
    if pad > count:
        mean = jnp.concatenate([mean, jnp.zeros((pad - count, 4 * DEPTH), BF)], axis=0)
    for part, (all_ref, tr) in enumerate(((kc, kt), (vc, vt))):
        cols = slice(part * DEPTH, (part + 1) * DEPTH)
        at = (2 * part + which) * DEPTH
        all_ref[:pad] = mean[:, at : at + DEPTH]
        all_ref[pad : pad + BLOCK] = prev_ref[:, cols]
        all_ref[pad + BLOCK :] = kv_ref[:, cols]
        tr[...] = all_ref[...].T
    dk[...] = jnp.zeros_like(dk)
    dv[...] = jnp.zeros_like(dv)

    def step(head, carry):
        for d, piece in enumerate(pieces):
            at = rows_of(d, small)
            qs[at, :] = piece[head, 0]
            gs[at, :] = piece[head, 1]

        for tile in range(BLOCK // TILE):
            rows = slice(tile * TILE, (tile + 1) * TILE)
            edge = pad + BLOCK + TILE * (tile + 1)
            q = qs[rows, :]
            s = dot(kc[:edge], q, 1, 1)
            s_sum = s[:pad]
            s_prev = s[pad : pad + BLOCK]
            s_diag = s[edge - TILE :]
            at = lax.broadcasted_iota(jnp.int32, (pad, TILE), 0)
            s_sum = jnp.where(at < ctx, s_sum, LOWEST)
            ki = lax.broadcasted_iota(jnp.int32, (TILE, TILE), 0)
            qi = lax.broadcasted_iota(jnp.int32, (TILE, TILE), 1)
            s_diag = jnp.where(ki <= qi, s_diag, LOWEST)
            slabs = [s_sum, s_prev, s_diag]
            if tile > 0:
                slabs.insert(2, s[pad + BLOCK : edge - TILE])
            tops = [jnp.max(x, axis=0, keepdims=True) for x in slabs]
            tops[1] = jnp.where(ctx > 0, tops[1], LOWEST)
            top = tops[0]
            for x in tops[1:]:
                top = jnp.maximum(top, x)
            shift = [top] * len(slabs)
            shift[1] = jnp.where(ctx > 0, top, -LOWEST)
            weights = [jnp.exp2((x - y) * coef) for x, y in zip(slabs, shift)]
            total = sum(jnp.sum(x, axis=0, keepdims=True) for x in weights)
            inv = 1.0 / total
            weight = jnp.concatenate(weights, axis=0)
            low = weight.astype(BF)
            attended = dot(vt[:, :edge], low, 1, 0) * inv
            os[rows, :] = attended.T.astype(BF)
            gt = (gs[rows, :].astype(F32).T * (16.0 * inv)).astype(BF)
            row_dot = jnp.sum(gt.astype(F32) * attended, axis=0, keepdims=True)
            back = dot(vc[:edge], gt, 1, 0)
            slope = (weight * (back - row_dot)).astype(BF)
            dqs[rows, :] = (dot(kt[:, :edge], slope, 1, 0) * scale).T.astype(BF)
            dk[:edge] += dot(slope, q, 1, 0)
            dv[:edge] += dot(low, gt, 1, 1)

        for d, out in enumerate(outs):
            at = rows_of(d, small)
            out[head, 0] = os[at, :]
            out[head, 1] = dqs[at, :]
        return carry

    lax.fori_loop(0, GROUP, step, 0)
    ds_ref[:, :DEPTH] = dk[:count] * scale
    ds_ref[:, DEPTH:] = dv[:count]
    edge_ref[:, :DEPTH] = (dk[pad : pad + BLOCK] * scale).astype(BF)
    edge_ref[:, DEPTH:] = dv[pad : pad + BLOCK].astype(BF)
    own_ref[:, :DEPTH] = dk[pad + BLOCK :] * scale
    own_ref[:, DEPTH:] = dv[pad + BLOCK :]


def attend(pieces, kv, prev, sums, which):
    parts = len(pieces)
    small = BLOCK // parts
    count = sums.shape[0]
    pad = max(16, -(-count // 16) * 16)
    width = pad + 2 * BLOCK
    outs = pl.pallas_call(
        lambda *refs: attend_kernel(parts, which, *refs),
        in_specs=[VM] * (parts + 3),
        out_specs=[VM] * (parts + 3),
        out_shape=[jax.ShapeDtypeStruct((GROUP, 2, small, DEPTH), BF)] * parts
        + [
            jax.ShapeDtypeStruct((BLOCK, 2 * DEPTH), BF),
            jax.ShapeDtypeStruct((BLOCK, 2 * DEPTH), F32),
            jax.ShapeDtypeStruct((count, 2 * DEPTH), F32),
        ],
        scratch_shapes=[
            pltpu.VMEM((width, DEPTH), BF),
            pltpu.VMEM((width, DEPTH), BF),
            pltpu.VMEM((DEPTH, width), BF),
            pltpu.VMEM((DEPTH, width), BF),
            pltpu.VMEM((width, DEPTH), F32),
            pltpu.VMEM((width, DEPTH), F32),
            pltpu.VMEM((BLOCK, DEPTH), BF),
            pltpu.VMEM((BLOCK, DEPTH), BF),
            pltpu.VMEM((BLOCK, DEPTH), BF),
            pltpu.VMEM((BLOCK, DEPTH), BF),
        ],
        compiler_params=pltpu.CompilerParams(vmem_limit_bytes=24 << 20),
        cost_estimate=pl.CostEstimate(
            flops=12 * GROUP * BLOCK * 2 * BLOCK * DEPTH,
            bytes_accessed=8 * BLOCK * GROUP * DEPTH,
            transcendentals=GROUP * BLOCK * 2 * BLOCK,
        ),
        name="attend",
    )(*pieces, kv, prev, sums)
    return outs[:parts], outs[parts], outs[parts + 1], outs[parts + 2]


def join_kernel(own_a, own_b, edge_a, edge_b, ds_ref, *outs):
    rows = outs[0].shape[0]
    total = jnp.sum(ds_ref[...], axis=0, keepdims=True) * (1.0 / BLOCK)
    for d, out in enumerate(outs):
        at = rows_of(d, rows)
        for g, (own, edge) in enumerate(((own_a, edge_a), (own_b, edge_b))):
            both = own[at, :] + edge[at, :].astype(F32)
            both = (both + total[:, 2 * g * DEPTH : 2 * (g + 1) * DEPTH]).astype(BF)
            out[:, g * DEPTH : (g + 1) * DEPTH] = both[:, :DEPTH]
            out[:, (2 + g) * DEPTH : (3 + g) * DEPTH] = both[:, DEPTH:]


def join(own, edge, ds, parts):
    return pl.pallas_call(
        join_kernel,
        in_specs=[VM] * 5,
        out_specs=[VM] * parts,
        out_shape=[jax.ShapeDtypeStruct((BLOCK // parts, 4 * DEPTH), BF)] * parts,
        compiler_params=ROOM, name="join",
    )(own[0], own[1], edge[0], edge[1], ds)


def unpack_kernel(*refs):
    parts = (len(refs) - 2) // 2
    o_ref, dq_ref = refs[-2:]
    for g in range(2):
        for d in range(parts):
            piece = refs[g * parts + d]
            for i in range(GROUP):
                at = pl.ds(pl.multiple_of(((2 * here(d) + g) * GROUP + i) * DEPTH, DEPTH), DEPTH)
                o_ref[:, at] = piece[i, 0]
                dq_ref[:, at] = piece[i, 1]


def unpack(a, b):
    parts = len(a)
    rows = a[0].shape[2]
    shape = jax.ShapeDtypeStruct((rows, parts * 2 * GROUP * DEPTH), BF)
    return pl.pallas_call(unpack_kernel, in_specs=[VM] * (2 * parts), out_shape=[shape, shape], compiler_params=ROOM, name="unpack")(*a, *b)


def finish_kernel(*refs):
    parts = len(refs) - 2
    dk_ref, dv_ref = refs[-2:]
    wide = 2 * DEPTH
    for d in range(parts):
        at = rows_of(d, wide)
        dk_ref[:, at] = refs[d][:, :wide]
        dv_ref[:, at] = refs[d][:, wide:]


def finish(pieces):
    parts = len(pieces)
    shape = jax.ShapeDtypeStruct((pieces[0].shape[0], parts * 2 * DEPTH), BF)
    return pl.pallas_call(
        finish_kernel, in_specs=[VM] * parts, out_shape=[shape, shape], compiler_params=ROOM, name="finish"
    )(*pieces)


def swap(pieces):
    parts = len(pieces)
    moved = []
    for d in range(1, parts):
        pairs = [(i, i ^ d) for i in range(parts)]
        moved.append(lax.ppermute(pieces[d], "head", pairs))
    return [pieces[0]] + moved


def layer(queries, keys, values, cotangent):
    rows = queries.shape[0]
    parts = lax.axis_size("head")
    blocks = lax.axis_size("ctx")
    assert rows * parts == BLOCK and parts * 2 == KEY_VALUE_HEADS
    forth = [(i, i + 1) for i in range(blocks - 1)]
    back = [(i + 1, i) for i in range(blocks - 1)]
    kv, sums = pack_kv(keys, values, parts, blocks)
    kv = swap(kv)
    pieces_a = pack(queries, cotangent, 0, parts)
    pieces_a = swap(pieces_a)
    pieces_b = pack(queries, cotangent, 1, parts)
    pieces_b = swap(pieces_b)
    kv_a, kv_b = gather(kv)
    prev_a = lax.ppermute(kv_a, "ctx", forth)
    prev_b = lax.ppermute(kv_b, "ctx", forth)
    sums = lax.all_to_all(
        sums.reshape(blocks * parts, 4 * DEPTH), ("ctx", "head"), 0, 0, tiled=True
    ).reshape(blocks, parts, 4 * DEPTH)
    out_a, edge_a, own_a, ds_a = attend(pieces_a, kv_a, prev_a, sums, 0)
    out_a = swap(out_a)
    edge_a = lax.ppermute(edge_a, "ctx", back)
    out_b, edge_b, own_b, ds_b = attend(pieces_b, kv_b, prev_b, sums, 1)
    edge_b = lax.ppermute(edge_b, "ctx", back)
    out_b = swap(out_b)
    ds = jnp.concatenate([ds_a, ds_b], axis=1)
    ds = lax.all_to_all(ds, "ctx", 0, 0, tiled=True)
    dkv = join((own_a, own_b), (edge_a, edge_b), ds, parts)
    dkv = swap(dkv)
    out, grad_queries = unpack(out_a, out_b)
    grad_keys, grad_values = finish(dkv)
    return out, grad_queries, grad_keys, grad_values


def solution(mesh):
    placed = P(("ctx", "head"), None)
    return jax.shard_map(
        layer, mesh=mesh, in_specs=(placed,) * 4, out_specs=(placed,) * 4, check_vma=False
    )
```

profile of v0, /device:TPU:9, one launch (start us, length us, event | category | flops | bytes accessed | tf_op | source)
XLA Modules:
  0.0 94.4 jit_solution(18248486498438377318)
XLA Ops:
  0.6 0.9 copy-done.4
  1.6 0.9 %copy-done.5 = bf16[128,1024]{1,0:T(8,128)(2,1)S(1)} copy-done((bf16[128,1024]{1,0:T(8,128)(2,1)S(1)}, bf16[128,1024]{1,0:T(8,128)(2,1)}, u32[]{:S(2)}) %copy-start.5) | copy-done | bytes 262168
  2.5 0.2 pack_kv.1
  2.7 0.7 collective-permute-start.3
  3.4 1.2 %collective-permute-start.4 = (bf16[128,512]{1,0:T(8,128)(2,1)S(1)}, bf16[128,512]{1,0:T(8,128)(2,1)S(1)}, u32[]{:S(2)}, u32[]{:S(2)}) collective-permute-start(bf16[128,512]{1,0:T(8,128)(2,1)S(1)} %get-tuple-element.47), channel_id=1, source_target_pairs={{0,2},{1,3},{2,0},{3,1},{4,6},{5,7},{6,4},{7,5},{8,10},{9,11},{10,... | collective-permute-start | bytes 393224 | tf_op jit(solution)/shard_map/ppermute | solution.py:299
  4.6 0.5 collective-permute-start.5
  5.1 1.2 %copy-done = bf16[128,4096]{1,0:T(8,128)(2,1)S(1)} copy-done((bf16[128,4096]{1,0:T(8,128)(2,1)S(1)}, bf16[128,4096]{1,0:T(8,128)(2,1)}, u32[]{:S(2)}) %copy-start) | copy-done | bytes 1048600
  6.4 1.2 %copy-done.2 = bf16[128,4096]{1,0:T(8,128)(2,1)S(1)} copy-done((bf16[128,4096]{1,0:T(8,128)(2,1)S(1)}, bf16[128,4096]{1,0:T(8,128)(2,1)}, u32[]{:S(2)}) %copy-start.2) | copy-done | bytes 1048600
  7.6 1.1 %pack.3 = (bf16[4,2,128,128]{3,2,1,0:T(8,128)(2,1)S(1)}, bf16[4,2,128,128]{3,2,1,0:T(8,128)(2,1)}, bf16[4,2,128,128]{3,2,1,0:T(8,128)(2,1)}, bf16[4,2,128,128]{3,2,1,0:T(8,128)(2,1)}) custom-call(bf16[128,4096]{1,0:T(8,128)(2,1)S(1)} %copy-done, bf16[128,4096]{1,0:T(8,128)(2,1)S(1)} %copy-done, bf16[128,4096]{1,0:T(8,128)(2,1)S(1)} %copy-done, ...), custom_call_target="tpu_custom_call" | custom-call | tf_op jit(solution)/shard_map/pack/pallas_call | solution.py:81
  8.6 0.2 collective-permute-start.10
  8.8 1.2 %collective-permute-start.11 = (bf16[4,2,128,128]{3,2,1,0:T(8,128)(2,1)}, bf16[4,2,128,128]{3,2,1,0:T(8,128)(2,1)S(1)}, u32[]{:S(2)}, u32[]{:S(2)}) collective-permute-start(bf16[4,2,128,128]{3,2,1,0:T(8,128)(2,1)} %get-tuple-element.57), channel_id=1, source_target_pairs={{0,2},{1,3},{2,0},{3,1},{4,6},{5,7},{6,4},{7,5},{8,10},{9,11},{10,... | collective-permute-start | bytes 786440 | tf_op jit(solution)/shard_map/ppermute | solution.py:299
  10.0 0.0 collective-permute-done.3.refs_1_
  10.0 0.8 collective-permute-start.12
  10.8 0.0 collective-permute-done.4.refs_2_
  10.8 0.7 collective-permute-done.5.refs_3_
  11.5 0.8 gather_kv.1
  12.3 3.1 %collective-permute-start.13 = (bf16[512,256]{1,0:T(8,128)(2,1)}, bf16[512,256]{1,0:T(8,128)(2,1)}, u32[]{:S(2)}, u32[]{:S(2)}) collective-permute-start(bf16[512,256]{1,0:T(8,128)(2,1)} %get-tuple-element.59.refs_4_), channel_id=1, source_target_pairs={{0,4},{4,8},{8,12},{12,16},{16,20},{20,24},{24,28},{1,5},{5,9},{9,... | collective-permute-start | bytes 786440 | tf_op jit(solution)/shard_map/ppermute | solution.py:318
  15.4 0.7 all_to_all.18
  16.1 5.1 %all-to-all-start = ((f32[32,1,512]{2,1,0:T(1,128)}), f32[32,1,512]{2,1,0:T(1,128)S(1)}, u32[]{:S(2)}, u32[]{:S(2)}) async-start(f32[32,1,512]{2,1,0:T(1,128)} %all_to_all.18), calls=%async_computation | async-start | bytes 131072 | tf_op jit(solution)/shard_map/all_to_all | solution.py:319
  21.3 1.0 %pack.2 = (bf16[4,2,128,128]{3,2,1,0:T(8,128)(2,1)S(1)}, bf16[4,2,128,128]{3,2,1,0:T(8,128)(2,1)}, bf16[4,2,128,128]{3,2,1,0:T(8,128)(2,1)S(1)}, bf16[4,2,128,128]{3,2,1,0:T(8,128)(2,1)S(1)}) custom-call(bf16[128,4096]{1,0:T(8,128)(2,1)S(1)} %copy-done.1, bf16[128,4096]{1,0:T(8,128)(2,1)S(1)} %copy-done.1, bf16[128,4096]{1,0:T(8,128)(2,1)S(1)} %copy-done.1, ...), custom_call_target="tpu_custom_call" | custom-call | tf_op jit(solution)/shard_map/pack/pallas_call | solution.py:81
  22.2 0.7 copy-done.6
  22.9 0.7 copy-done.8
  23.6 0.7 copy-done.10
  24.3 0.4 collective-permute-start
  24.7 2.1 %all-to-all-done = f32[32,1,512]{2,1,0:T(1,128)S(1)} async-done(((f32[32,1,512]{2,1,0:T(1,128)}), f32[32,1,512]{2,1,0:T(1,128)S(1)}, u32[]{:S(2)}, u32[]{:S(2)}) %all-to-all-start) | async-done | bytes 65568 | tf_op jit(solution)/shard_map/all_to_all | solution.py:319
  26.9 0.2 reduce
  27.0 0.0 collective-permute-done.10.refs_1_
  27.1 0.8 collective-permute-start.1
  27.9 0.0 collective-permute-done.11.refs_2_
  27.9 1.9 %collective-permute-start.2 = (bf16[4,2,128,128]{3,2,1,0:T(8,128)(2,1)S(1)}, bf16[4,2,128,128]{3,2,1,0:T(8,128)(2,1)S(1)}, u32[]{:S(2)}, u32[]{:S(2)}) collective-permute-start(bf16[4,2,128,128]{3,2,1,0:T(8,128)(2,1)S(1)} %copy-done.9), channel_id=1, source_target_pairs={{0,3},{1,2},{2,1},{3,0},{4,7},{5,6},{6,5},{7,4},{8,11},{9,10},{10,... | collective-permute-start | bytes 786440 | tf_op jit(solution)/shard_map/ppermute | solution.py:299
  29.8 0.0 collective-permute-done.12.refs_3_
  29.8 2.2 %collective-permute-start.6 = (bf16[512,256]{1,0:T(8,128)(2,1)S(1)}, bf16[512,256]{1,0:T(8,128)(2,1)S(1)}, u32[]{:S(2)}, u32[]{:S(2)}) collective-permute-start(bf16[512,256]{1,0:T(8,128)(2,1)S(1)} %get-tuple-element.49.refs_4_), channel_id=1, source_target_pairs={{0,4},{4,8},{8,12},{12,16},{16,20},{20,24},{24,28},{1,5},{5,9},{9,... | collective-permute-start | bytes 786440 | tf_op jit(solution)/shard_map/ppermute | solution.py:317
  32.0 0.0 collective-permute-done.13.refs_5_
  32.0 0.0 copy-start.7
  32.0 12.6 %attend.3 = (bf16[4,2,128,128]{3,2,1,0:T(8,128)(2,1)S(1)}, bf16[4,2,128,128]{3,2,1,0:T(8,128)(2,1)S(1)}, bf16[4,2,128,128]{3,2,1,0:T(8,128)(2,1)S(1)}, bf16[4,2,...) custom-call(bf16[4,2,128,128]{3,2,1,0:T(8,128)(2,1)S(1)} %get-tuple-e, ...), custom_call_target="tpu_custom_call" | custom-call | flops 3221225472 | bytes 2097152 | tf_op jit(solution)/shard_map/attend/pallas_call | solution.py:202
  44.7 4.0 %collective-permute-start.18 = (bf16[512,256]{1,0:T(8,128)(2,1)S(1)}, bf16[512,256]{1,0:T(8,128)(2,1)S(1)}, u32[]{:S(2)}, u32[]{:S(2)}) collective-permute-start(bf16[512,256]{1,0:T(8,128)(2,1)S(1)} %get-tuple-element.69), channel_id=1, source_target_pairs={{4,0},{8,4},{12,8},{16,12},{20,16},{24,20},{28,24},{5,1},{9,5},{13... | collective-permute-start | bytes 786440 | tf_op jit(solution)/shard_map/ppermute | solution.py:326
  48.6 0.0 collective-permute-done.refs_1_
  48.6 0.0 collective-permute-done.1.refs_2_
  48.7 0.0 collective-permute-done.2.refs_3_
  48.7 0.0 collective-permute-done.6.refs_5_
  48.7 11.5 %attend.2 = (bf16[4,2,128,128]{3,2,1,0:T(8,128)(2,1)S(1)}, bf16[4,2,128,128]{3,2,1,0:T(8,128)(2,1)S(1)}, bf16[4,2,128,128]{3,2,1,0:T(8,128)(2,1)S(1)}, bf16[4,2,...) custom-call(bf16[4,2,128,128]{3,2,1,0:T(8,128)(2,1)S(1)} %copy-done.7, ...), custom_call_target="tpu_custom_call" | custom-call | flops 3221225472 | bytes 2097152 | tf_op jit(solution)/shard_map/attend/pallas_call | solution.py:202
  60.2 2.2 %collective-permute-start.17 = (bf16[512,256]{1,0:T(8,128)(2,1)S(1)}, bf16[512,256]{1,0:T(8,128)(2,1)S(1)}, u32[]{:S(2)}, u32[]{:S(2)}) collective-permute-start(bf16[512,256]{1,0:T(8,128)(2,1)S(1)} %get-tuple-element.68), channel_id=1, source_target_pairs={{4,0},{8,4},{12,8},{16,12},{20,16},{24,20},{28,24},{5,1},{9,5},{13... | collective-permute-start | bytes 786440 | tf_op jit(solution)/shard_map/ppermute | solution.py:324
  62.4 0.7 collective-permute-start.14
  63.1 0.4 collective-permute-start.15
  63.5 1.3 %collective-permute-start.16 = (bf16[4,2,128,128]{3,2,1,0:T(8,128)(2,1)S(1)}, bf16[4,2,128,128]{3,2,1,0:T(8,128)(2,1)S(1)}, u32[]{:S(2)}, u32[]{:S(2)}) collective-permute-start(bf16[4,2,128,128]{3,2,1,0:T(8,128)(2,1)S(1)} %get-tuple-element.63), channel_id=1, source_target_pairs={{0,3},{1,2},{2,1},{3,0},{4,7},{5,6},{6,5},{7,4},{8,11},{9,10},{10,... | collective-permute-start | bytes 786440 | tf_op jit(solution)/shard_map/ppermute | solution.py:299
  64.8 0.0 collective-permute-done.18.edge_b
  64.8 0.2 collective-permute-start.7
  64.9 5.3 %collective-permute-done.17.edge_a = bf16[512,256]{1,0:T(8,128)(2,1)S(1)} collective-permute-done((bf16[512,256]{1,0:T(8,128)(2,1)S(1)}, bf16[512,256]{1,0:T(8,128)(2,1)S(1)}, u32[]{:S(2)}, u32[]{:S(2)}) %collective-permute-start.17) | collective-permute-done | bytes 262176 | tf_op jit(solution)/shard_map/ppermute | solution.py:324
  70.2 0.0 collective-permute-start.8
  70.2 0.0 collective-permute-done.14.refs_5_
  70.2 2.3 %collective-permute-start.9 = (bf16[4,2,128,128]{3,2,1,0:T(8,128)(2,1)S(1)}, bf16[4,2,128,128]{3,2,1,0:T(8,128)(2,1)S(1)}, u32[]{:S(2)}, u32[]{:S(2)}) collective-permute-start(bf16[4,2,128,128]{3,2,1,0:T(8,128)(2,1)S(1)} %get-tuple-element.54), channel_id=1, source_target_pairs={{0,3},{1,2},{2,1},{3,0},{4,7},{5,6},{6,5},{7,4},{8,11},{9,10},{10,... | collective-permute-start | bytes 786440 | tf_op jit(solution)/shard_map/ppermute | solution.py:299
  72.5 7.0 %all_to_all.21 = f32[8,1,512]{2,1,0:T(1,128)S(1)} all-to-all(f32[8,1,512]{2,1,0:T(1,128)S(1)} %copy.9), channel_id=1, replica_groups=mesh['ctx'=8,'head'=4] {'ctx'}, dimensions={0} | all-to-all | bytes 32768 | tf_op jit(solution)/shard_map/all_to_all | solution.py:329
  79.5 0.1 join.1
  79.6 0.9 collective-permute-start.19
  80.5 0.0 collective-permute-done.16.refs_7_
  80.5 0.7 collective-permute-start.20
  81.2 0.0 collective-permute-done.7.refs_1_
  81.2 1.0 %collective-permute-start.21 = (bf16[128,512]{1,0:T(8,128)(2,1)S(1)}, bf16[128,512]{1,0:T(8,128)(2,1)S(1)}, u32[]{:S(2)}, u32[]{:S(2)}) collective-permute-start(bf16[128,512]{1,0:T(8,128)(2,1)S(1)} %get-tuple-element.75), channel_id=1, source_target_pairs={{0,3},{1,2},{2,1},{3,0},{4,7},{5,6},{6,5},{7,4},{8,11},{9,10},{10,... | collective-permute-start | bytes 393224 | tf_op jit(solution)/shard_map/ppermute | solution.py:299
  82.3 0.0 collective-permute-done.8.refs_2_
  82.3 6.2 %collective-permute-done.9.refs_3_ = bf16[4,2,128,128]{3,2,1,0:T(8,128)(2,1)S(1)} collective-permute-done((bf16[4,2,128,128]{3,2,1,0:T(8,128)(2,1)S(1)}, bf16[4,2,128,128]{3,2,1,0:T(8,128)(2,1)S(1)}, u32[]{:S(2)}, u32[]{:S(2)}) %collective-permute-start.9) | collective-permute-done | bytes 262176 | tf_op jit(solution)/shard_map/ppermute | solution.py:299
  88.5 1.9 %unpack.1 = (bf16[128,4096]{1,0:T(8,128)(2,1)}, bf16[128,4096]{1,0:T(8,128)(2,1)}) custom-call(bf16[4,2,128,128]{3,2,1,0:T(8,128)(2,1)S(1)} %get-tuple-element.51.refs_0_, bf16[4,2,128,128]{3,2,1,0:T(8,128)(2,1)S(1)} %collective-permute-done.7.refs_1_, bf16[4,2,128,128]{3,2,1,0:T(8,128)(2,1)S(1)} %collective-permute-done.8.refs_2_, ...), custom_call_target="tpu_custom_call" | custom-call | tf_op jit(solution)/shard_map/unpack/pallas_call | solution.py:273
  90.4 0.1 collective-permute-done.20.refs_2_
  90.5 3.1 %collective-permute-done.21.refs_3_ = bf16[128,512]{1,0:T(8,128)(2,1)S(1)} collective-permute-done((bf16[128,512]{1,0:T(8,128)(2,1)S(1)}, bf16[128,512]{1,0:T(8,128)(2,1)S(1)}, u32[]{:S(2)}, u32[]{:S(2)}) %collective-permute-start.21) | collective-permute-done | bytes 131104 | tf_op jit(solution)/shard_map/ppermute | solution.py:299
  93.6 0.9 finish.1
  (20 shorter events, 0.1 us)
Async XLA Ops:
  0.6 1.0 %copy-start.4 = (bf16[128,1024]{1,0:T(8,128)(2,1)S(1)}, bf16[128,1024]{1,0:T(8,128)(2,1)}, u32[]{:S(2)}) copy-start(bf16[128,1024]{1,0:T(8,128)(2,1)} %k_ref.1) | copy-start | bytes 786436
  1.6 0.9 %copy-start.5 = (bf16[128,1024]{1,0:T(8,128)(2,1)S(1)}, bf16[128,1024]{1,0:T(8,128)(2,1)}, u32[]{:S(2)}) copy-start(bf16[128,1024]{1,0:T(8,128)(2,1)} %v_ref.1) | copy-start | bytes 786436
  2.7 7.3 %collective-permute-start.3 = (bf16[128,512]{1,0:T(8,128)(2,1)S(1)}, bf16[128,512]{1,0:T(8,128)(2,1)S(1)}, u32[]{:S(2)}, u32[]{:S(2)}) collective-permute-start(bf16[128,512]{1,0:T(8,128)(2,1)S(1)} %get-tuple-element.46), channel_id=1, source_target_pairs={{0,1},{1,0},{2,3},{3,2},{4,5},{5,4},{6,7},{7,6},{8,9},{9,8},{10,11... | collective-permute-start | bytes 393224 | tf_op jit(solution)/shard_map/ppermute | solution.py:299
  3.4 7.4 %collective-permute-start.4 = (bf16[128,512]{1,0:T(8,128)(2,1)S(1)}, bf16[128,512]{1,0:T(8,128)(2,1)S(1)}, u32[]{:S(2)}, u32[]{:S(2)}) collective-permute-start(bf16[128,512]{1,0:T(8,128)(2,1)S(1)} %get-tuple-element.47), channel_id=1, source_target_pairs={{0,2},{1,3},{2,0},{3,1},{4,6},{5,7},{6,4},{7,5},{8,10},{9,11},{10,... | collective-permute-start | bytes 393224 | tf_op jit(solution)/shard_map/ppermute | solution.py:299
  4.6 6.8 %collective-permute-start.5 = (bf16[128,512]{1,0:T(8,128)(2,1)S(1)}, bf16[128,512]{1,0:T(8,128)(2,1)S(1)}, u32[]{:S(2)}, u32[]{:S(2)}) collective-permute-start(bf16[128,512]{1,0:T(8,128)(2,1)S(1)} %get-tuple-element.48), channel_id=1, source_target_pairs={{0,3},{1,2},{2,1},{3,0},{4,7},{5,6},{6,5},{7,4},{8,11},{9,10},{10,... | collective-permute-start | bytes 393224 | tf_op jit(solution)/shard_map/ppermute | solution.py:299
  5.1 1.2 %copy-start = (bf16[128,4096]{1,0:T(8,128)(2,1)S(1)}, bf16[128,4096]{1,0:T(8,128)(2,1)}, u32[]{:S(2)}) copy-start(bf16[128,4096]{1,0:T(8,128)(2,1)} %refs_3_.3) | copy-start | bytes 3145732
  6.4 1.2 %copy-start.2 = (bf16[128,4096]{1,0:T(8,128)(2,1)S(1)}, bf16[128,4096]{1,0:T(8,128)(2,1)}, u32[]{:S(2)}) copy-start(bf16[128,4096]{1,0:T(8,128)(2,1)} %refs_7_.3) | copy-start | bytes 3145732
  7.6 13.7 %copy-start.1 = (bf16[128,4096]{1,0:T(8,128)(2,1)S(1)}, bf16[128,4096]{1,0:T(8,128)(2,1)}, u32[]{:S(2)}) copy-start(bf16[128,4096]{1,0:T(8,128)(2,1)} %refs_3_.3) | copy-start | bytes 3145732
  7.6 13.7 %copy-start.3 = (bf16[128,4096]{1,0:T(8,128)(2,1)S(1)}, bf16[128,4096]{1,0:T(8,128)(2,1)}, u32[]{:S(2)}) copy-start(bf16[128,4096]{1,0:T(8,128)(2,1)} %refs_7_.3) | copy-start | bytes 3145732
  8.6 18.4 %collective-permute-start.10 = (bf16[4,2,128,128]{3,2,1,0:T(8,128)(2,1)}, bf16[4,2,128,128]{3,2,1,0:T(8,128)(2,1)S(1)}, u32[]{:S(2)}, u32[]{:S(2)}) collective-permute-start(bf16[4,2,128,128]{3,2,1,0:T(8,128)(2,1)} %get-tuple-element.56), channel_id=1, source_target_pairs={{0,1},{1,0},{2,3},{3,2},{4,5},{5,4},{6,7},{7,6},{8,9},{9,8},{10,11... | collective-permute-start | bytes 786440 | tf_op jit(solution)/shard_map/ppermute | solution.py:299
  8.8 19.1 %collective-permute-start.11 = (bf16[4,2,128,128]{3,2,1,0:T(8,128)(2,1)}, bf16[4,2,128,128]{3,2,1,0:T(8,128)(2,1)S(1)}, u32[]{:S(2)}, u32[]{:S(2)}) collective-permute-start(bf16[4,2,128,128]{3,2,1,0:T(8,128)(2,1)} %get-tuple-element.57), channel_id=1, source_target_pairs={{0,2},{1,3},{2,0},{3,1},{4,6},{5,7},{6,4},{7,5},{8,10},{9,11},{10,... | collective-permute-start | bytes 786440 | tf_op jit(solution)/shard_map/ppermute | solution.py:299
  10.0 19.8 %collective-permute-start.12 = (bf16[4,2,128,128]{3,2,1,0:T(8,128)(2,1)}, bf16[4,2,128,128]{3,2,1,0:T(8,128)(2,1)S(1)}, u32[]{:S(2)}, u32[]{:S(2)}) collective-permute-start(bf16[4,2,128,128]{3,2,1,0:T(8,128)(2,1)} %get-tuple-element.58), channel_id=1, source_target_pairs={{0,3},{1,2},{2,1},{3,0},{4,7},{5,6},{6,5},{7,4},{8,11},{9,10},{10,... | collective-permute-start | bytes 786440 | tf_op jit(solution)/shard_map/ppermute | solution.py:299
  12.3 19.7 %collective-permute-start.13 = (bf16[512,256]{1,0:T(8,128)(2,1)}, bf16[512,256]{1,0:T(8,128)(2,1)}, u32[]{:S(2)}, u32[]{:S(2)}) collective-permute-start(bf16[512,256]{1,0:T(8,128)(2,1)} %get-tuple-element.59.refs_4_), channel_id=1, source_target_pairs={{0,4},{4,8},{8,12},{12,16},{16,20},{20,24},{24,28},{1,5},{5,9},{9,... | collective-permute-start | bytes 786440 | tf_op jit(solution)/shard_map/ppermute | solution.py:318
  16.1 10.7 %all-to-all-start = ((f32[32,1,512]{2,1,0:T(1,128)}), f32[32,1,512]{2,1,0:T(1,128)S(1)}, u32[]{:S(2)}, u32[]{:S(2)}) async-start(f32[32,1,512]{2,1,0:T(1,128)} %all_to_all.18), calls=%async_computation | async-start | bytes 131072 | tf_op jit(solution)/shard_map/all_to_all | solution.py:319
  22.2 0.7 copy-start.6
  22.9 0.7 copy-start.8
  23.6 0.7 copy-start.10
  24.3 3.6 %copy-start.9 = (bf16[4,2,128,128]{3,2,1,0:T(8,128)(2,1)S(1)}, bf16[4,2,128,128]{3,2,1,0:T(8,128)(2,1)}, u32[]{:S(2)}) copy-start(bf16[4,2,128,128]{3,2,1,0:T(8,128)(2,1)} %copy-done.8) | copy-start | bytes 786436
  24.3 24.3 %collective-permute-start = (bf16[4,2,128,128]{3,2,1,0:T(8,128)(2,1)}, bf16[4,2,128,128]{3,2,1,0:T(8,128)(2,1)S(1)}, u32[]{:S(2)}, u32[]{:S(2)}) collective-permute-start(bf16[4,2,128,128]{3,2,1,0:T(8,128)(2,1)} %get-tuple-element.42), channel_id=1, source_target_pairs={{0,1},{1,0},{2,3},{3,2},{4,5},{5,4},{6,7},{7,6},{8,9},{9,8},{10,11... | collective-permute-start | bytes 786440 | tf_op jit(solution)/shard_map/ppermute | solution.py:299
  27.1 21.6 %collective-permute-start.1 = (bf16[4,2,128,128]{3,2,1,0:T(8,128)(2,1)}, bf16[4,2,128,128]{3,2,1,0:T(8,128)(2,1)S(1)}, u32[]{:S(2)}, u32[]{:S(2)}) collective-permute-start(bf16[4,2,128,128]{3,2,1,0:T(8,128)(2,1)} %copy-done.10), channel_id=1, source_target_pairs={{0,2},{1,3},{2,0},{3,1},{4,6},{5,7},{6,4},{7,5},{8,10},{9,11},{10,... | collective-permute-start | bytes 786440 | tf_op jit(solution)/shard_map/ppermute | solution.py:299
  27.9 20.8 %collective-permute-start.2 = (bf16[4,2,128,128]{3,2,1,0:T(8,128)(2,1)S(1)}, bf16[4,2,128,128]{3,2,1,0:T(8,128)(2,1)S(1)}, u32[]{:S(2)}, u32[]{:S(2)}) collective-permute-start(bf16[4,2,128,128]{3,2,1,0:T(8,128)(2,1)S(1)} %copy-done.9), channel_id=1, source_target_pairs={{0,3},{1,2},{2,1},{3,0},{4,7},{5,6},{6,5},{7,4},{8,11},{9,10},{10,... | collective-permute-start | bytes 786440 | tf_op jit(solution)/shard_map/ppermute | solution.py:299
  29.8 18.9 %collective-permute-start.6 = (bf16[512,256]{1,0:T(8,128)(2,1)S(1)}, bf16[512,256]{1,0:T(8,128)(2,1)S(1)}, u32[]{:S(2)}, u32[]{:S(2)}) collective-permute-start(bf16[512,256]{1,0:T(8,128)(2,1)S(1)} %get-tuple-element.49.refs_4_), channel_id=1, source_target_pairs={{0,4},{4,8},{8,12},{12,16},{16,20},{20,24},{24,28},{1,5},{5,9},{9,... | collective-permute-start | bytes 786440 | tf_op jit(solution)/shard_map/ppermute | solution.py:317
  32.0 16.7 %copy-start.7 = (bf16[4,2,128,128]{3,2,1,0:T(8,128)(2,1)S(1)}, bf16[4,2,128,128]{3,2,1,0:T(8,128)(2,1)}, u32[]{:S(2)}) copy-start(bf16[4,2,128,128]{3,2,1,0:T(8,128)(2,1)} %copy-done.6) | copy-start | bytes 786436
  44.7 20.1 %collective-permute-start.18 = (bf16[512,256]{1,0:T(8,128)(2,1)S(1)}, bf16[512,256]{1,0:T(8,128)(2,1)S(1)}, u32[]{:S(2)}, u32[]{:S(2)}) collective-permute-start(bf16[512,256]{1,0:T(8,128)(2,1)S(1)} %get-tuple-element.69), channel_id=1, source_target_pairs={{4,0},{8,4},{12,8},{16,12},{20,16},{24,20},{28,24},{5,1},{9,5},{13... | collective-permute-start | bytes 786440 | tf_op jit(solution)/shard_map/ppermute | solution.py:326
  60.2 10.0 %collective-permute-start.17 = (bf16[512,256]{1,0:T(8,128)(2,1)S(1)}, bf16[512,256]{1,0:T(8,128)(2,1)S(1)}, u32[]{:S(2)}, u32[]{:S(2)}) collective-permute-start(bf16[512,256]{1,0:T(8,128)(2,1)S(1)} %get-tuple-element.68), channel_id=1, source_target_pairs={{4,0},{8,4},{12,8},{16,12},{20,16},{24,20},{28,24},{5,1},{9,5},{13... | collective-permute-start | bytes 786440 | tf_op jit(solution)/shard_map/ppermute | solution.py:324
  62.4 7.8 %collective-permute-start.14 = (bf16[4,2,128,128]{3,2,1,0:T(8,128)(2,1)S(1)}, bf16[4,2,128,128]{3,2,1,0:T(8,128)(2,1)S(1)}, u32[]{:S(2)}, u32[]{:S(2)}) collective-permute-start(bf16[4,2,128,128]{3,2,1,0:T(8,128)(2,1)S(1)} %get-tuple-element.61), channel_id=1, source_target_pairs={{0,1},{1,0},{2,3},{3,2},{4,5},{5,4},{6,7},{7,6},{8,9},{9,8},{10,11... | collective-permute-start | bytes 786440 | tf_op jit(solution)/shard_map/ppermute | solution.py:299
  63.1 16.5 %collective-permute-start.15 = (bf16[4,2,128,128]{3,2,1,0:T(8,128)(2,1)S(1)}, bf16[4,2,128,128]{3,2,1,0:T(8,128)(2,1)S(1)}, u32[]{:S(2)}, u32[]{:S(2)}) collective-permute-start(bf16[4,2,128,128]{3,2,1,0:T(8,128)(2,1)S(1)} %get-tuple-element.62), channel_id=1, source_target_pairs={{0,2},{1,3},{2,0},{3,1},{4,6},{5,7},{6,4},{7,5},{8,10},{9,11},{10,... | collective-permute-start | bytes 786440 | tf_op jit(solution)/shard_map/ppermute | solution.py:299
  63.5 17.0 %collective-permute-start.16 = (bf16[4,2,128,128]{3,2,1,0:T(8,128)(2,1)S(1)}, bf16[4,2,128,128]{3,2,1,0:T(8,128)(2,1)S(1)}, u32[]{:S(2)}, u32[]{:S(2)}) collective-permute-start(bf16[4,2,128,128]{3,2,1,0:T(8,128)(2,1)S(1)} %get-tuple-element.63), channel_id=1, source_target_pairs={{0,3},{1,2},{2,1},{3,0},{4,7},{5,6},{6,5},{7,4},{8,11},{9,10},{10,... | collective-permute-start | bytes 786440 | tf_op jit(solution)/shard_map/ppermute | solution.py:299
  64.8 16.5 %collective-permute-start.7 = (bf16[4,2,128,128]{3,2,1,0:T(8,128)(2,1)S(1)}, bf16[4,2,128,128]{3,2,1,0:T(8,128)(2,1)S(1)}, u32[]{:S(2)}, u32[]{:S(2)}) collective-permute-start(bf16[4,2,128,128]{3,2,1,0:T(8,128)(2,1)S(1)} %get-tuple-element.52), channel_id=1, source_target_pairs={{0,1},{1,0},{2,3},{3,2},{4,5},{5,4},{6,7},{7,6},{8,9},{9,8},{10,11... | collective-permute-start | bytes 786440 | tf_op jit(solution)/shard_map/ppermute | solution.py:299
  70.2 12.1 %collective-permute-start.8 = (bf16[4,2,128,128]{3,2,1,0:T(8,128)(2,1)S(1)}, bf16[4,2,128,128]{3,2,1,0:T(8,128)(2,1)S(1)}, u32[]{:S(2)}, u32[]{:S(2)}) collective-permute-start(bf16[4,2,128,128]{3,2,1,0:T(8,128)(2,1)S(1)} %get-tuple-element.53), channel_id=1, source_target_pairs={{0,2},{1,3},{2,0},{3,1},{4,6},{5,7},{6,4},{7,5},{8,10},{9,11},{10,... | collective-permute-start | bytes 786440 | tf_op jit(solution)/shard_map/ppermute | solution.py:299
  70.2 18.3 %collective-permute-start.9 = (bf16[4,2,128,128]{3,2,1,0:T(8,128)(2,1)S(1)}, bf16[4,2,128,128]{3,2,1,0:T(8,128)(2,1)S(1)}, u32[]{:S(2)}, u32[]{:S(2)}) collective-permute-start(bf16[4,2,128,128]{3,2,1,0:T(8,128)(2,1)S(1)} %get-tuple-element.54), channel_id=1, source_target_pairs={{0,3},{1,2},{2,1},{3,0},{4,7},{5,6},{6,5},{7,4},{8,11},{9,10},{10,... | collective-permute-start | bytes 786440 | tf_op jit(solution)/shard_map/ppermute | solution.py:299
  79.6 10.8 %collective-permute-start.19 = (bf16[128,512]{1,0:T(8,128)(2,1)S(1)}, bf16[128,512]{1,0:T(8,128)(2,1)S(1)}, u32[]{:S(2)}, u32[]{:S(2)}) collective-permute-start(bf16[128,512]{1,0:T(8,128)(2,1)S(1)} %get-tuple-element.73), channel_id=1, source_target_pairs={{0,1},{1,0},{2,3},{3,2},{4,5},{5,4},{6,7},{7,6},{8,9},{9,8},{10,11... | collective-permute-start | bytes 393224 | tf_op jit(solution)/shard_map/ppermute | solution.py:299
  80.5 10.0 %collective-permute-start.20 = (bf16[128,512]{1,0:T(8,128)(2,1)S(1)}, bf16[128,512]{1,0:T(8,128)(2,1)S(1)}, u32[]{:S(2)}, u32[]{:S(2)}) collective-permute-start(bf16[128,512]{1,0:T(8,128)(2,1)S(1)} %get-tuple-element.74), channel_id=1, source_target_pairs={{0,2},{1,3},{2,0},{3,1},{4,6},{5,7},{6,4},{7,5},{8,10},{9,11},{10,... | collective-permute-start | bytes 393224 | tf_op jit(solution)/shard_map/ppermute | solution.py:299
  81.2 12.3 %collective-permute-start.21 = (bf16[128,512]{1,0:T(8,128)(2,1)S(1)}, bf16[128,512]{1,0:T(8,128)(2,1)S(1)}, u32[]{:S(2)}, u32[]{:S(2)}) collective-permute-start(bf16[128,512]{1,0:T(8,128)(2,1)S(1)} %get-tuple-element.75), channel_id=1, source_target_pairs={{0,3},{1,2},{2,1},{3,0},{4,7},{5,6},{6,5},{7,4},{8,11},{9,10},{10,... | collective-permute-start | bytes 393224 | tf_op jit(solution)/shard_map/ppermute | solution.py:299
where the time goes:
time: 94.9 us; the launch traced here: 94.4 us
  starting transfers between devices  31.7 us (33%)
  Pallas kernels  30 us (32%)
  waiting for transfers between devices  17.6 us (19%)
  local copies, waits for them, and re-layouts  7.22 us (8%)
  blocking collectives  6.96 us (7%)
    pallas_call x2, Pallas kernels, attend(): pl.pallas_call(lambda *refs: attend_kernel(parts, which, *refs), in_specs...  24.2 us
    ppermute x18, starting transfers between devices, swap(): moved.append(lax.ppermute(pieces[d], 'head', pairs))  15.1 us
    ppermute x18, waiting for transfers between devices, swap(): moved.append(lax.ppermute(pieces[d], 'head', pairs))  10.2 us
    all_to_all x1, blocking collectives, layer(): ds = lax.all_to_all(ds, 'ctx', 0, 0, tiled=True)  6.96 us
    unnamed x23, local copies, waits for them, and re-layouts  6.47 us
    ppermute x1, waiting for transfers between devices, layer(): edge_a = lax.ppermute(edge_a, 'ctx', back)  5.26 us
    all_to_all x1, starting transfers between devices, layer(): lax.all_to_all(sums.reshape(blocks * parts, 4 * DEPTH), ('ctx', 'head'),...  5.09 us
    ppermute x1, starting transfers between devices, layer(): edge_b = lax.ppermute(edge_b, 'ctx', back)  3.96 us
  transfers between devices with their start and end apart: 23, of which 6 were waited for; matrix products, arithmetic and copies ran while one was open for 0% of the time, Pallas kernels for 31%

commit v1 on v0

v1 whole, which is shorter than its diff:
```python
import jax
import jax.numpy as jnp
from jax import lax
from jax.experimental import pallas as pl
from jax.experimental.pallas import tpu as pltpu
from jax.sharding import PartitionSpec as P


QUERY_HEADS = 32
KEY_VALUE_HEADS = 8
DEPTH = 128
BLOCK = 512
TILE = 256
GROUP = QUERY_HEADS // KEY_VALUE_HEADS
LOWEST = -1e30
LOG2E = 1.4426950408889634

BF = jnp.bfloat16
F32 = jnp.float32


def dot(a, b, ca, cb):
    return lax.dot_general(a, b, (((ca,), (cb,)), ((), ())), preferred_element_type=F32)


VM = pl.BlockSpec(memory_space=pltpu.VMEM)
HB = pl.BlockSpec(memory_space=pltpu.HBM)
ROOM = pltpu.CompilerParams(vmem_limit_bytes=12 << 20)


def here(d):
    return lax.axis_index("head") ^ d


def rows_of(d, size):
    return pl.ds(pl.multiple_of(here(d) * size, size), size)


def run(copies):
    for copy in copies:
        copy.start()
    for copy in copies:
        copy.wait()


def cols_of(start, size):
    return pl.ds(pl.multiple_of(start * size, size), size)


def pack_kv_kernel(k_ref, v_ref, *outs):
    sems, outs = outs[-1], outs[:-1]
    wide = 2 * DEPTH
    copies = []
    for d, out in enumerate(outs):
        cols = cols_of(here(d), wide)
        for i, ref in enumerate((k_ref, v_ref)):
            half = out.at[:, pl.ds(i * wide, wide)]
            copies.append(pltpu.make_async_copy(ref.at[:, cols], half, sems.at[2 * d + i]))
    run(copies)


def pack_kv(k, v, parts):
    rows = k.shape[0]
    return pl.pallas_call(
        pack_kv_kernel,
        in_specs=[HB] * 2,
        out_specs=[VM] * parts,
        out_shape=[jax.ShapeDtypeStruct((rows, 4 * DEPTH), BF)] * parts,
        scratch_shapes=[pltpu.SemaphoreType.DMA((2 * parts,))],
        compiler_params=ROOM,
        name="pack_kv",
    )(k, v)


def pack_kernel(q_ref, g_ref, *outs):
    sems, outs = outs[-1], outs[:-1]
    parts = len(outs) // 2
    copies = []
    for which in range(2):
        for d in range(parts):
            cols = cols_of(2 * here(d) + which, GROUP * DEPTH)
            for i, ref in enumerate((q_ref, g_ref)):
                out = outs[which * parts + d].at[i]
                copies.append(pltpu.make_async_copy(ref.at[:, cols], out, sems.at[len(copies)]))
    run(copies)


def pack(q, g, parts):
    outs = pl.pallas_call(
        pack_kernel,
        in_specs=[HB] * 2,
        out_specs=[VM] * (2 * parts),
        out_shape=[jax.ShapeDtypeStruct((2, q.shape[0], GROUP * DEPTH), BF)] * (2 * parts),
        scratch_shapes=[pltpu.SemaphoreType.DMA((4 * parts,))],
        compiler_params=ROOM,
        name="pack",
    )(q, g)
    return outs[:parts], outs[parts:]


def gather_kernel(*refs):
    a_ref, b_ref, sums_ref = refs[-3:]
    rows = refs[0].shape[0]
    total = jnp.zeros((1, 4 * DEPTH), F32)
    for d, piece in enumerate(refs[:-3]):
        at = rows_of(d, rows)
        for which, out in enumerate((a_ref, b_ref)):
            out[at, :DEPTH] = piece[:, which * DEPTH : (which + 1) * DEPTH]
            out[at, DEPTH:] = piece[:, (2 + which) * DEPTH : (3 + which) * DEPTH]
        total = total + jnp.sum(piece[...].astype(F32), axis=0, keepdims=True)
    for block in range(sums_ref.shape[0]):
        sums_ref[block] = total


def gather(pieces, blocks):
    return pl.pallas_call(
        gather_kernel,
        in_specs=[VM] * len(pieces),
        out_specs=[VM] * 3,
        out_shape=[jax.ShapeDtypeStruct((BLOCK, 2 * DEPTH), BF)] * 2
        + [jax.ShapeDtypeStruct((blocks, 1, 4 * DEPTH), F32)],
        compiler_params=ROOM,
        name="gather_kv",
    )(*pieces)


def unflatten(refs):
    return (*refs[:10], refs[10:12], refs[12:14], refs[14], refs[15])


def attend_kernel(parts, which, *refs):
    pieces = refs[:parts]
    kv_ref, prev_ref, sums_ref = refs[parts : parts + 3]
    outs = refs[parts + 3 : 2 * parts + 3]
    edge_ref, own_ref, ds_ref = refs[2 * parts + 3 : 2 * parts + 6]
    kc, vc, kt, vt, dk, dv, qs, gs, os, dqs, sbufs, lbufs, dbuf, tops = unflatten(refs[2 * parts + 6 :])
    ctx = lax.axis_index("ctx")
    scale = DEPTH ** (-0.5)
    coef = scale * LOG2E
    count = sums_ref.shape[0]
    pad = kc.shape[0] - 2 * BLOCK
    small = BLOCK // parts

    mean = jnp.concatenate([sums_ref[c] for c in range(count)], axis=0)
    mean = (mean * (1.0 / BLOCK)).astype(BF)
    if pad > count:
        mean = jnp.concatenate([mean, jnp.zeros((pad - count, 4 * DEPTH), BF)], axis=0)
    for part, (all_ref, tr) in enumerate(((kc, kt), (vc, vt))):
        cols = slice(part * DEPTH, (part + 1) * DEPTH)
        at = (2 * part + which) * DEPTH
        all_ref[:pad] = mean[:, at : at + DEPTH]
        all_ref[pad : pad + BLOCK] = prev_ref[:, cols]
        all_ref[pad + BLOCK :] = kv_ref[:, cols]
        tr[...] = all_ref[...].T
    dk[...] = jnp.zeros_like(dk)
    dv[...] = jnp.zeros_like(dv)

    def extent(tile):
        return pad + BLOCK + TILE * (tile + 1)

    def chunks(tile):
        cuts = [0] + list(range(pad + TILE, extent(tile) + 1, TILE))
        return list(zip(cuts[:-1], cuts[1:]))

    def fetch(head):
        for d, piece in enumerate(pieces):
            at = rows_of(d, small)
            qs[at, :] = piece[0, :, cols_of(head, DEPTH)]
            gs[at, :] = piece[1, :, cols_of(head, DEPTH)]

    def rows_in(tile):
        return slice(tile * TILE, (tile + 1) * TILE)

    def scores(tile):
        state = dict(own=jnp.full((1, TILE), LOWEST, F32), prev=jnp.full((1, TILE), LOWEST, F32))

        def part(lo, hi):
            def go():
                s = dot(kc[lo:hi], qs[rows_in(tile), :], 1, 1)
                if lo == 0:
                    at = lax.broadcasted_iota(jnp.int32, (pad, TILE), 0)
                    first = jnp.where(at < ctx, s[:pad], LOWEST)
                    sbufs[tile][:pad] = first
                    state["own"] = jnp.maximum(state["own"], jnp.max(first, axis=0, keepdims=True))
                    s = s[pad:]
                if hi == extent(tile):
                    ki = lax.broadcasted_iota(jnp.int32, (TILE, TILE), 0)
                    qi = lax.broadcasted_iota(jnp.int32, (TILE, TILE), 1)
                    s = jnp.where(ki <= qi, s, LOWEST)
                sbufs[tile][max(lo, pad) : hi] = s
                name = "prev" if hi <= pad + BLOCK else "own"
                state[name] = jnp.maximum(state[name], jnp.max(s, axis=0, keepdims=True))
                if hi == extent(tile):
                    prev = jnp.where(ctx > 0, state["prev"], LOWEST)
                    tops[tile] = jnp.maximum(state["own"], prev)

            return go

        return [part(lo, hi) for lo, hi in chunks(tile)]

    def weigh(tile, state):
        def part(lo, hi):
            def go():
                top = tops[tile]
                behind = jnp.where(ctx > 0, top, -LOWEST)
                edges = [(lo, pad, top), (pad, hi, behind)] if lo == 0 else [
                    (lo, hi, behind if hi <= pad + BLOCK else top)
                ]
                for a, b, shift in edges:
                    w = jnp.exp2((sbufs[tile][a:b] - shift) * coef)
                    sbufs[tile][a:b] = w
                    lbufs[tile][a:b] = w.astype(BF)
                    total = jnp.sum(w, axis=0, keepdims=True)
                    state["total"] = total + state["total"] if "total" in state else total

            return go

        return [part(lo, hi) for lo, hi in chunks(tile)]

    def gradients(tile, state):
        edge = extent(tile)
        rows = rows_in(tile)

        def out():
            inv = 1.0 / state["total"]
            attended = dot(vt[:, :edge], lbufs[tile][:edge], 1, 0) * inv
            os[rows, :] = attended.T.astype(BF)
            gt = (gs[rows, :].astype(F32).T * (16.0 * inv)).astype(BF)
            state["gt"] = gt
            state["dot"] = jnp.sum(gt.astype(F32) * attended, axis=0, keepdims=True)

        def part(lo, hi):
            def go():
                back = dot(vc[lo:hi], state["gt"], 1, 0)
                dbuf[lo:hi] = (sbufs[tile][lo:hi] * (back - state["dot"])).astype(BF)

            return go

        def query():
            dqs[rows, :] = (dot(kt[:, :edge], dbuf[:edge], 1, 0) * scale).T.astype(BF)

        def store(lo, hi):
            def go():
                dv[lo:hi] += dot(lbufs[tile][lo:hi], state["gt"], 1, 1)
                dk[lo:hi] += dot(dbuf[lo:hi], qs[rows, :], 1, 0)

            return go

        steps = [out] + [part(lo, hi) for lo, hi in chunks(tile)] + [query]
        return steps + [store(lo, hi) for lo, hi in chunks(tile)]

    def weave(*stages):
        order = []
        for n, stage in enumerate(stages):
            order += [((i + 0.5) / len(stage), n, i, go) for i, go in enumerate(stage)]
        for item in sorted(order, key=lambda x: x[:3]):
            item[3]()

    fetch(0)
    weave(scores(0))

    def step(head, carry):
        first, second = {}, {}
        weave(scores(1), weigh(0, first))
        weave(gradients(0, first), weigh(1, second))
        weave(gradients(1, second))
        for d, out in enumerate(outs):
            at = rows_of(d, small)
            out[0, :, cols_of(head, DEPTH)] = os[at, :]
            out[1, :, cols_of(head, DEPTH)] = dqs[at, :]
        fetch(jnp.minimum(head + 1, GROUP - 1))
        weave(scores(0))
        return carry

    lax.fori_loop(0, GROUP, step, 0)
    ds_ref[:, :DEPTH] = dk[:count] * scale
    ds_ref[:, DEPTH:] = dv[:count]
    edge_ref[:, :DEPTH] = (dk[pad : pad + BLOCK] * scale).astype(BF)
    edge_ref[:, DEPTH:] = dv[pad : pad + BLOCK].astype(BF)
    own_ref[:, :DEPTH] = dk[pad + BLOCK :] * scale
    own_ref[:, DEPTH:] = dv[pad + BLOCK :]


def attend(pieces, kv, prev, sums, which):
    parts = len(pieces)
    small = BLOCK // parts
    count = sums.shape[0]
    pad = max(16, -(-count // 16) * 16)
    width = pad + 2 * BLOCK
    outs = pl.pallas_call(
        lambda *refs: attend_kernel(parts, which, *refs),
        in_specs=[VM] * (parts + 3),
        out_specs=[VM] * (parts + 3),
        out_shape=[jax.ShapeDtypeStruct((2, small, GROUP * DEPTH), BF)] * parts
        + [
            jax.ShapeDtypeStruct((BLOCK, 2 * DEPTH), BF),
            jax.ShapeDtypeStruct((BLOCK, 2 * DEPTH), F32),
            jax.ShapeDtypeStruct((count, 2 * DEPTH), F32),
        ],
        scratch_shapes=[
            pltpu.VMEM((width, DEPTH), BF),
            pltpu.VMEM((width, DEPTH), BF),
            pltpu.VMEM((DEPTH, width), BF),
            pltpu.VMEM((DEPTH, width), BF),
            pltpu.VMEM((width, DEPTH), F32),
            pltpu.VMEM((width, DEPTH), F32),
            pltpu.VMEM((BLOCK, DEPTH), BF),
            pltpu.VMEM((BLOCK, DEPTH), BF),
            pltpu.VMEM((BLOCK, DEPTH), BF),
            pltpu.VMEM((BLOCK, DEPTH), BF),
            pltpu.VMEM((width - TILE, TILE), F32),
            pltpu.VMEM((width, TILE), F32),
            pltpu.VMEM((width - TILE, TILE), BF),
            pltpu.VMEM((width, TILE), BF),
            pltpu.VMEM((width, TILE), BF),
            pltpu.VMEM((2, 1, TILE), F32),
        ],
        compiler_params=pltpu.CompilerParams(vmem_limit_bytes=24 << 20),
        cost_estimate=pl.CostEstimate(
            flops=12 * GROUP * BLOCK * 2 * BLOCK * DEPTH,
            bytes_accessed=8 * BLOCK * GROUP * DEPTH,
            transcendentals=GROUP * BLOCK * 2 * BLOCK,
        ),
        name="attend",
    )(*pieces, kv, prev, sums)
    return outs[:parts], outs[parts], outs[parts + 1], outs[parts + 2]


def join_kernel(own_a, own_b, edge_a, edge_b, *outs):
    rows = outs[0].shape[0]
    for d, out in enumerate(outs):
        at = rows_of(d, rows)
        for g, (own, edge) in enumerate(((own_a, edge_a), (own_b, edge_b))):
            both = (own[at, :] + edge[at, :].astype(F32)).astype(BF)
            out[:, g * DEPTH : (g + 1) * DEPTH] = both[:, :DEPTH]
            out[:, (2 + g) * DEPTH : (3 + g) * DEPTH] = both[:, DEPTH:]


def join(own, edge, parts):
    return pl.pallas_call(
        join_kernel,
        in_specs=[VM] * 4,
        out_specs=[VM] * parts,
        out_shape=[jax.ShapeDtypeStruct((BLOCK // parts, 4 * DEPTH), BF)] * parts,
        compiler_params=ROOM,
        name="join",
    )(own[0], own[1], edge[0], edge[1])


def spread_kernel(a_ref, b_ref, out_ref):
    blocks = a_ref.shape[0]
    parts = out_ref.shape[0] // blocks
    for block in range(blocks):
        for g, ref in enumerate((a_ref, b_ref)):
            row = ref[block : block + 1, :]
            for i in range(2):
                at = (2 * i + g) * DEPTH
                part = row[:, i * DEPTH : (i + 1) * DEPTH]
                for h in range(parts):
                    out_ref[block * parts + h, :, at : at + DEPTH] = part


def spread(a, b, parts):
    return pl.pallas_call(
        spread_kernel,
        in_specs=[VM] * 2,
        out_specs=VM,
        out_shape=jax.ShapeDtypeStruct((a.shape[0] * parts, 1, 4 * DEPTH), F32),
        compiler_params=ROOM,
        name="spread",
    )(a, b)


def unpack_kernel(*refs):
    sems, outs, pieces = refs[-1], refs[-3:-1], refs[:-3]
    parts = len(pieces) // 2
    copies = []
    for n, piece in enumerate(pieces):
        cols = cols_of(2 * here(n % parts) + n // parts, GROUP * DEPTH)
        for i, out in enumerate(outs):
            copies.append(
                pltpu.make_async_copy(piece.at[i], out.at[:, cols], sems.at[len(copies)])
            )
    run(copies)


def unpack(a, b):
    parts = len(a)
    rows = a[0].shape[1]
    shape = jax.ShapeDtypeStruct((rows, parts * 2 * GROUP * DEPTH), BF)
    return pl.pallas_call(
        unpack_kernel,
        in_specs=[VM] * (2 * parts),
        out_specs=[HB] * 2,
        out_shape=[shape, shape],
        scratch_shapes=[pltpu.SemaphoreType.DMA((4 * parts,))],
        compiler_params=ROOM,
        name="unpack",
    )(*a, *b)


def finish_kernel(*refs):
    ds_ref, dk_out, dv_out, dk_ref, dv_ref, sems = refs[-6:]
    pieces = refs[:-6]
    parts = len(pieces)
    wide = 2 * DEPTH
    for d, piece in enumerate(pieces):
        total = sum(ds_ref[c * parts + here(d)] for c in range(ds_ref.shape[0] // parts))
        full = (piece[...].astype(F32) + total * (1.0 / BLOCK)).astype(BF)
        cols = cols_of(here(d), wide)
        dk_ref[:, cols] = full[:, :wide]
        dv_ref[:, cols] = full[:, wide:]
    pairs = ((dk_ref, dk_out), (dv_ref, dv_out))
    run([pltpu.make_async_copy(a, b, sems.at[i]) for i, (a, b) in enumerate(pairs)])


def finish(pieces, ds):
    parts = len(pieces)
    rows = pieces[0].shape[0]
    shape = (rows, parts * 2 * DEPTH)
    return pl.pallas_call(
        finish_kernel,
        in_specs=[VM] * (parts + 1),
        out_specs=[HB] * 2,
        out_shape=[jax.ShapeDtypeStruct(shape, BF)] * 2,
        scratch_shapes=[pltpu.VMEM(shape, BF)] * 2 + [pltpu.SemaphoreType.DMA((2,))],
        compiler_params=ROOM,
        name="finish",
    )(*pieces, ds)


def swap(pieces):
    parts = len(pieces)
    moved = []
    for d in range(1, parts):
        pairs = [(i, i ^ d) for i in range(parts)]
        moved.append(lax.ppermute(pieces[d], "head", pairs))
    return [pieces[0]] + moved


def layer(queries, keys, values, cotangent):
    rows = queries.shape[0]
    parts = lax.axis_size("head")
    blocks = lax.axis_size("ctx")
    assert rows * parts == BLOCK and parts * 2 == KEY_VALUE_HEADS
    forth = [(i, i + 1) for i in range(blocks - 1)]
    back = [(i + 1, i) for i in range(blocks - 1)]
    queries, keys, values, cotangent = [
        pltpu.with_memory_space_constraint(x, pltpu.HBM)
        for x in (queries, keys, values, cotangent)
    ]
    kv = pack_kv(keys, values, parts)
    kv = swap(kv)
    pieces_a, pieces_b = pack(queries, cotangent, parts)
    pieces_a = swap(pieces_a)
    pieces_b = swap(pieces_b)
    kv_a, kv_b, sums = gather(kv, blocks)
    prev_a = lax.ppermute(kv_a, "ctx", forth)
    prev_b = lax.ppermute(kv_b, "ctx", forth)
    sums = lax.all_to_all(sums, "ctx", 0, 0, tiled=True)
    out_a, edge_a, own_a, ds_a = attend(pieces_a, kv_a, prev_a, sums, 0)
    out_a = swap(out_a)
    edge_a = lax.ppermute(edge_a, "ctx", back)
    out_b, edge_b, own_b, ds_b = attend(pieces_b, kv_b, prev_b, sums, 1)
    edge_b = lax.ppermute(edge_b, "ctx", back)
    out_b = swap(out_b)
    ds = spread(ds_a, ds_b, parts)
    ds = lax.all_to_all(ds, ("ctx", "head"), 0, 0, tiled=True)
    dkv = join((own_a, own_b), (edge_a, edge_b), parts)
    dkv = swap(dkv)
    out, grad_queries = unpack(out_a, out_b)
    grad_keys, grad_values = finish(dkv, ds)
    return out, grad_queries, grad_keys, grad_values


def solution(mesh):
    placed = P(("ctx", "head"), None)
    return jax.shard_map(
        layer, mesh=mesh, in_specs=(placed,) * 4, out_specs=(placed,) * 4, check_vma=False
    )
```

time: 94.9 us -> 87.6 us (0.923)
  the two profiles are of different devices: /device:TPU:9 before, /device:TPU:0 now
where the time goes in v1:
time: 87.6 us; the launch traced here: 87.1 us
  starting transfers between devices  36.5 us (42%)
  Pallas kernels  26.4 us (30%)
  waiting for transfers between devices  20.1 us (23%)
  local copies, waits for them, and re-layouts  3.3 us (4%)
    pallas_call x2, Pallas kernels, attend(): pl.pallas_call(lambda *refs: attend_kernel(parts, which, *refs), in_specs...  18.2 us
    ppermute x18, starting transfers between devices, swap(): moved.append(lax.ppermute(pieces[d], 'head', pairs))  13.7 us
    all_to_all x1, waiting for transfers between devices, layer(): ds = lax.all_to_all(ds, ('ctx', 'head'), 0, 0, tiled=True)  8.01 us
    all_to_all x1, starting transfers between devices, layer(): ds = lax.all_to_all(ds, ('ctx', 'head'), 0, 0, tiled=True)  7.99 us
    ppermute x1, waiting for transfers between devices, layer(): edge_a = lax.ppermute(edge_a, 'ctx', back)  6.46 us
    ppermute x18, waiting for transfers between devices, swap(): moved.append(lax.ppermute(pieces[d], 'head', pairs))  4.83 us
    all_to_all x1, starting transfers between devices, layer(): sums = lax.all_to_all(sums, 'ctx', 0, 0, tiled=True)  4.18 us
    ppermute x1, starting transfers between devices, layer(): prev_b = lax.ppermute(kv_b, 'ctx', forth)  4.12 us
  transfers between devices with their start and end apart: 24, of which 6 were waited for; matrix products, arithmetic and copies ran while one was open for 0% of the time, Pallas kernels for 28%

profile of v1, /device:TPU:0, one launch (start us, length us, event | category | flops | bytes accessed | tf_op | source)
XLA Modules:
  0.0 87.1 jit_solution(10626704816690018176)
XLA Ops:
  0.6 1.1 %pack_kv.1 = (bf16[128,512]{1,0:T(8,128)(2,1)S(1)}, bf16[128,512]{1,0:T(8,128)(2,1)S(1)}, bf16[128,512]{1,0:T(8,128)(2,1)S(1)}, bf16[128,512]{1,0:T(8,128)(2,1)S(1)}) custom-call(bf16[128,1024]{1,0:T(8,128)(2,1)} %k_ref.1, bf16[128,1024]{1,0:T(8,128)(2,1)} %v_ref.1), custom_call_target="tpu_custom_call" | custom-call | tf_op jit(solution)/shard_map/pack_kv/pallas_call | solution.py:64
  1.8 0.6 collective-permute-start.3
  2.3 2.6 %collective-permute-start.4 = (bf16[128,512]{1,0:T(8,128)(2,1)S(1)}, bf16[128,512]{1,0:T(8,128)(2,1)S(1)}, u32[]{:S(2)}, u32[]{:S(2)}) collective-permute-start(bf16[128,512]{1,0:T(8,128)(2,1)S(1)} %get-tuple-element.47), channel_id=1, source_target_pairs={{0,2},{1,3},{2,0},{3,1},{4,6},{5,7},{6,4},{7,5},{8,10},{9,11},{10,... | collective-permute-start | bytes 393224 | tf_op jit(solution)/shard_map/ppermute | solution.py:437
  4.9 0.0 collective-permute-start.5
  4.9 2.4 %pack.1 = (bf16[2,128,512]{2,1,0:T(8,128)(2,1)S(1)}, bf16[2,128,512]{2,1,0:T(8,128)(2,1)S(1)}, bf16[2,128,512]{2,1,0:T(8,128)(2,1)S(1)}, bf16[2,128,512]{2,1,0:T...) custom-call(bf16[128,4096]{1,0:T(8,128)(2,1)} %q_ref.1, ...), custom_call_target="tpu_custom_call" | custom-call | tf_op jit(solution)/shard_map/pack/pallas_call | solution.py:89
  7.4 0.2 collective-permute-start.10
  7.6 1.9 %collective-permute-start.11 = (bf16[2,128,512]{2,1,0:T(8,128)(2,1)}, bf16[2,128,512]{2,1,0:T(8,128)(2,1)S(1)}, u32[]{:S(2)}, u32[]{:S(2)}) collective-permute-start(bf16[2,128,512]{2,1,0:T(8,128)(2,1)} %get-tuple-element.57), channel_id=1, source_target_pairs={{0,2},{1,3},{2,0},{3,1},{4,6},{5,7},{6,4},{7,5},{8,10},{9,11},{10,... | collective-permute-start | bytes 786440 | tf_op jit(solution)/shard_map/ppermute | solution.py:437
  9.6 0.0 collective-permute-done.3.refs_1_
  9.6 0.0 collective-permute-start.12
  9.6 0.0 collective-permute-done.4.refs_2_
  9.6 2.0 %collective-permute-done.5.refs_3_ = bf16[128,512]{1,0:T(8,128)(2,1)S(1)} collective-permute-done((bf16[128,512]{1,0:T(8,128)(2,1)S(1)}, bf16[128,512]{1,0:T(8,128)(2,1)S(1)}, u32[]{:S(2)}, u32[]{:S(2)}) %collective-permute-start.5) | collective-permute-done | bytes 131104 | tf_op jit(solution)/shard_map/ppermute | solution.py:437
  11.6 0.8 gather_kv.1
  12.4 4.1 %collective-permute-start.13 = (bf16[512,256]{1,0:T(8,128)(2,1)S(1)}, bf16[512,256]{1,0:T(8,128)(2,1)}, u32[]{:S(2)}, u32[]{:S(2)}) collective-permute-start(bf16[512,256]{1,0:T(8,128)(2,1)S(1)} %get-tuple-element.59.refs_4_), channel_id=1, source_target_pairs={{0,4},{4,8},{8,12},{12,16},{16,20},{20,24},{24,28},{1,5},{5,9},{9,... | collective-permute-start | bytes 786440 | tf_op jit(solution)/shard_map/ppermute | solution.py:459
  16.5 0.0 copy-start
  16.5 0.7 copy-done
  17.2 4.2 %all-to-all-start = ((f32[8,1,512]{2,1,0:T(1,128)}), f32[8,1,512]{2,1,0:T(1,128)S(1)}, u32[]{:S(2)}, u32[]{:S(2)}) async-start(f32[8,1,512]{2,1,0:T(1,128)} %get-tuple-element.50), calls=%async_computation | async-start | bytes 32768 | tf_op jit(solution)/shard_map/all_to_all | solution.py:460
  21.4 0.3 collective-permute-start
  21.6 0.0 collective-permute-done.10.refs_1_
  21.6 1.5 %collective-permute-start.1 = (bf16[2,128,512]{2,1,0:T(8,128)(2,1)S(1)}, bf16[2,128,512]{2,1,0:T(8,128)(2,1)S(1)}, u32[]{:S(2)}, u32[]{:S(2)}) collective-permute-start(bf16[2,128,512]{2,1,0:T(8,128)(2,1)S(1)} %get-tuple-element.43), channel_id=1, source_target_pairs={{0,2},{1,3},{2,0},{3,1},{4,6},{5,7},{6,4},{7,5},{8,10},{9,11},{10,... | collective-permute-start | bytes 786440 | tf_op jit(solution)/shard_map/ppermute | solution.py:437
  23.1 0.0 collective-permute-done.11.refs_2_
  23.1 0.1 collective-permute-start.2
  23.2 0.0 collective-permute-done.12.refs_3_
  23.2 3.9 %collective-permute-start.6 = (bf16[512,256]{1,0:T(8,128)(2,1)S(1)}, bf16[512,256]{1,0:T(8,128)(2,1)S(1)}, u32[]{:S(2)}, u32[]{:S(2)}) collective-permute-start(bf16[512,256]{1,0:T(8,128)(2,1)S(1)} %get-tuple-element.49.refs_4_), channel_id=1, source_target_pairs={{0,4},{4,8},{8,12},{12,16},{16,20},{20,24},{24,28},{1,5},{5,9},{9,... | collective-permute-start | bytes 786440 | tf_op jit(solution)/shard_map/ppermute | solution.py:458
  27.2 0.8 all-to-all-done.refs_6_
  28.0 0.0 collective-permute-done.13.refs_5_
  28.0 0.0 copy-start.1
  28.0 0.9 %copy-done.1 = bf16[512,256]{1,0:T(8,128)(2,1)S(1)} copy-done((bf16[512,256]{1,0:T(8,128)(2,1)S(1)}, bf16[512,256]{1,0:T(8,128)(2,1)}, u32[]{:S(2)}) %copy-start.1) | copy-done | bytes 262168
  28.9 9.1 %attend.3 = (bf16[2,128,512]{2,1,0:T(8,128)(2,1)S(1)}, bf16[2,128,512]{2,1,0:T(8,128)(2,1)S(1)}, bf16[2,128,512]{2,1,0:T(8,128)(2,1)S(1)}, bf16[2,128,512]{2,1,0...) custom-call(bf16[2,128,512]{2,1,0:T(8,128)(2,1)S(1)} %get-tuple-element.55.refs_0_, ...), custom_call_target="tpu_custom_call" | custom-call | flops 3221225472 | bytes 2097152 | tf_op jit(solution)/shard_map/attend/pallas_call | solution.py:290
  38.0 1.3 %collective-permute-start.18 = (bf16[512,256]{1,0:T(8,128)(2,1)S(1)}, bf16[512,256]{1,0:T(8,128)(2,1)S(1)}, u32[]{:S(2)}, u32[]{:S(2)}) collective-permute-start(bf16[512,256]{1,0:T(8,128)(2,1)S(1)} %get-tuple-element.69), channel_id=1, source_target_pairs={{4,0},{8,4},{12,8},{16,12},{20,16},{24,20},{28,24},{5,1},{9,5},{13... | collective-permute-start | bytes 786440 | tf_op jit(solution)/shard_map/ppermute | solution.py:465
  39.3 0.0 collective-permute-done.refs_1_
  39.3 0.0 collective-permute-done.1.refs_2_
  39.3 0.0 collective-permute-done.2.refs_3_
  39.4 0.0 collective-permute-done.6.refs_5_
  39.4 0.0 copy-start.2
  39.4 0.7 copy-done.2
  40.1 0.9 %copy-done.3 = bf16[512,256]{1,0:T(8,128)(2,1)S(1)} copy-done((bf16[512,256]{1,0:T(8,128)(2,1)S(1)}, bf16[512,256]{1,0:T(8,128)(2,1)}, u32[]{:S(2)}) %copy-start.3) | copy-done | bytes 262168
  41.0 9.1 %attend.2 = (bf16[2,128,512]{2,1,0:T(8,128)(2,1)S(1)}, bf16[2,128,512]{2,1,0:T(8,128)(2,1)S(1)}, bf16[2,128,512]{2,1,0:T(8,128)(2,1)S(1)}, bf16[2,128,512]{2,1,0...) custom-call(bf16[2,128,512]{2,1,0:T(8,128)(2,1)S(1)} %get-tuple-element.41.refs_0_, ...), custom_call_target="tpu_custom_call" | custom-call | flops 3221225472 | bytes 2097152 | tf_op jit(solution)/shard_map/attend/pallas_call | solution.py:290
  50.2 1.3 %collective-permute-start.17 = (bf16[512,256]{1,0:T(8,128)(2,1)S(1)}, bf16[512,256]{1,0:T(8,128)(2,1)S(1)}, u32[]{:S(2)}, u32[]{:S(2)}) collective-permute-start(bf16[512,256]{1,0:T(8,128)(2,1)S(1)} %get-tuple-element.68), channel_id=1, source_target_pairs={{4,0},{8,4},{12,8},{16,12},{20,16},{24,20},{28,24},{5,1},{9,5},{13... | collective-permute-start | bytes 786440 | tf_op jit(solution)/shard_map/ppermute | solution.py:463
  51.5 0.1 collective-permute-start.14
  51.5 1.6 %collective-permute-start.15 = (bf16[2,128,512]{2,1,0:T(8,128)(2,1)S(1)}, bf16[2,128,512]{2,1,0:T(8,128)(2,1)S(1)}, u32[]{:S(2)}, u32[]{:S(2)}) collective-permute-start(bf16[2,128,512]{2,1,0:T(8,128)(2,1)S(1)} %get-tuple-element.62), channel_id=1, source_target_pairs={{0,2},{1,3},{2,0},{3,1},{4,6},{5,7},{6,4},{7,5},{8,10},{9,11},{10,... | collective-permute-start | bytes 786440 | tf_op jit(solution)/shard_map/ppermute | solution.py:437
  53.1 0.3 collective-permute-start.16
  53.4 0.0 collective-permute-done.18.edge_b
  53.4 0.4 collective-permute-start.7
  53.8 6.5 %collective-permute-done.17.edge_a = bf16[512,256]{1,0:T(8,128)(2,1)S(1)} collective-permute-done((bf16[512,256]{1,0:T(8,128)(2,1)S(1)}, bf16[512,256]{1,0:T(8,128)(2,1)S(1)}, u32[]{:S(2)}, u32[]{:S(2)}) %collective-permute-start.17) | collective-permute-done | bytes 262176 | tf_op jit(solution)/shard_map/ppermute | solution.py:463
  60.2 1.5 %collective-permute-start.8 = (bf16[2,128,512]{2,1,0:T(8,128)(2,1)S(1)}, bf16[2,128,512]{2,1,0:T(8,128)(2,1)S(1)}, u32[]{:S(2)}, u32[]{:S(2)}) collective-permute-start(bf16[2,128,512]{2,1,0:T(8,128)(2,1)S(1)} %get-tuple-element.53), channel_id=1, source_target_pairs={{0,2},{1,3},{2,0},{3,1},{4,6},{5,7},{6,4},{7,5},{8,10},{9,11},{10,... | collective-permute-start | bytes 786440 | tf_op jit(solution)/shard_map/ppermute | solution.py:437
  61.7 0.0 collective-permute-done.14.refs_5_
  61.7 0.0 collective-permute-start.9
  61.7 0.7 join.1
  62.4 0.0 collective-permute-done.15.refs_6_
  62.4 0.6 collective-permute-start.19
  63.1 2.4 %collective-permute-done.16.refs_7_ = bf16[2,128,512]{2,1,0:T(8,128)(2,1)S(1)} collective-permute-done((bf16[2,128,512]{2,1,0:T(8,128)(2,1)S(1)}, bf16[2,128,512]{2,1,0:T(8,128)(2,1)S(1)}, u32[]{:S(2)}, u32[]{:S(2)}) %collective-permute-start.16) | collective-permute-done | bytes 262176 | tf_op jit(solution)/shard_map/ppermute | solution.py:437
  65.4 1.4 %collective-permute-start.20 = (bf16[128,512]{1,0:T(8,128)(2,1)S(1)}, bf16[128,512]{1,0:T(8,128)(2,1)S(1)}, u32[]{:S(2)}, u32[]{:S(2)}) collective-permute-start(bf16[128,512]{1,0:T(8,128)(2,1)S(1)} %get-tuple-element.72), channel_id=1, source_target_pairs={{0,2},{1,3},{2,0},{3,1},{4,6},{5,7},{6,4},{7,5},{8,10},{9,11},{10,... | collective-permute-start | bytes 393224 | tf_op jit(solution)/shard_map/ppermute | solution.py:437
  66.8 0.0 collective-permute-done.7.refs_1_
  66.8 0.7 collective-permute-start.21
  67.6 0.7 spread.1
  68.2 8.0 %all-to-all-start.1 = ((f32[32,1,512]{2,1,0:T(1,128)}), f32[32,1,512]{2,1,0:T(1,128)S(1)}, u32[]{:S(2)}, u32[]{:S(2)}) async-start(f32[32,1,512]{2,1,0:T(1,128)} %spread.1), calls=%async_computation.1 | async-start | bytes 131072 | tf_op jit(solution)/shard_map/all_to_all | solution.py:468
  76.2 0.0 collective-permute-done.8.refs_2_
  76.3 0.4 collective-permute-done.9.refs_3_
  76.7 1.4 %unpack.1 = (bf16[128,4096]{1,0:T(8,128)(2,1)}, bf16[128,4096]{1,0:T(8,128)(2,1)}) custom-call(bf16[2,128,512]{2,1,0:T(8,128)(2,1)S(1)} %get-tuple-element.51.refs_0_, bf16[2,128,512]{2,1,0:T(8,128)(2,1)S(1)} %collective-permute-done.7.refs_1_, bf16[2,128,512]{2,1,0:T(8,128)(2,1)S(1)} %collective-permute-done.8.refs_2_, ...), custom_call_target="tpu_custom_call" | custom-call | tf_op jit(solution)/shard_map/unpack/pallas_call | solution.py:391
  78.1 8.0 %all-to-all-done.1.refs_4_ = f32[32,1,512]{2,1,0:T(1,128)S(1)} async-done(((f32[32,1,512]{2,1,0:T(1,128)}), f32[32,1,512]{2,1,0:T(1,128)S(1)}, u32[]{:S(2)}, u32[]{:S(2)}) %all-to-all-start.1) | async-done | bytes 65568 | tf_op jit(solution)/shard_map/all_to_all | solution.py:468
  86.1 0.0 collective-permute-done.19.refs_1_
  86.1 0.0 collective-permute-done.20.refs_2_
  86.1 0.0 collective-permute-done.21.refs_3_
  86.1 0.9 %finish.1 = (bf16[128,1024]{1,0:T(8,128)(2,1)}, bf16[128,1024]{1,0:T(8,128)(2,1)}) custom-call(bf16[128,512]{1,0:T(8,128)(2,1)S(1)} %get-tuple-element.70.refs_0_, bf16[128,512]{1,0:T(8,128)(2,1)S(1)} %collective-permute-done.19.refs_1_, bf16[128,512]{1,0:T(8,128)(2,1)S(1)} %collective-permute-done.20.refs_2_, ...), custom_call_target="tpu_custom_call" | custom-call | tf_op jit(solution)/shard_map/finish/pallas_call | solution.py:421
  (1 shorter events, 0.0 us)
Async XLA Ops:
  1.8 7.8 %collective-permute-start.3 = (bf16[128,512]{1,0:T(8,128)(2,1)S(1)}, bf16[128,512]{1,0:T(8,128)(2,1)S(1)}, u32[]{:S(2)}, u32[]{:S(2)}) collective-permute-start(bf16[128,512]{1,0:T(8,128)(2,1)S(1)} %get-tuple-element.46), channel_id=1, source_target_pairs={{0,1},{1,0},{2,3},{3,2},{4,5},{5,4},{6,7},{7,6},{8,9},{9,8},{10,11... | collective-permute-start | bytes 393224 | tf_op jit(solution)/shard_map/ppermute | solution.py:437
  2.3 7.2 %collective-permute-start.4 = (bf16[128,512]{1,0:T(8,128)(2,1)S(1)}, bf16[128,512]{1,0:T(8,128)(2,1)S(1)}, u32[]{:S(2)}, u32[]{:S(2)}) collective-permute-start(bf16[128,512]{1,0:T(8,128)(2,1)S(1)} %get-tuple-element.47), channel_id=1, source_target_pairs={{0,2},{1,3},{2,0},{3,1},{4,6},{5,7},{6,4},{7,5},{8,10},{9,11},{10,... | collective-permute-start | bytes 393224 | tf_op jit(solution)/shard_map/ppermute | solution.py:437
  4.9 6.7 %collective-permute-start.5 = (bf16[128,512]{1,0:T(8,128)(2,1)S(1)}, bf16[128,512]{1,0:T(8,128)(2,1)S(1)}, u32[]{:S(2)}, u32[]{:S(2)}) collective-permute-start(bf16[128,512]{1,0:T(8,128)(2,1)S(1)} %get-tuple-element.48), channel_id=1, source_target_pairs={{0,3},{1,2},{2,1},{3,0},{4,7},{5,6},{6,5},{7,4},{8,11},{9,10},{10,... | collective-permute-start | bytes 393224 | tf_op jit(solution)/shard_map/ppermute | solution.py:437
  7.4 14.2 %collective-permute-start.10 = (bf16[2,128,512]{2,1,0:T(8,128)(2,1)S(1)}, bf16[2,128,512]{2,1,0:T(8,128)(2,1)S(1)}, u32[]{:S(2)}, u32[]{:S(2)}) collective-permute-start(bf16[2,128,512]{2,1,0:T(8,128)(2,1)S(1)} %get-tuple-element.56), channel_id=1, source_target_pairs={{0,1},{1,0},{2,3},{3,2},{4,5},{5,4},{6,7},{7,6},{8,9},{9,8},{10,11... | collective-permute-start | bytes 786440 | tf_op jit(solution)/shard_map/ppermute | solution.py:437
  7.6 15.5 %collective-permute-start.11 = (bf16[2,128,512]{2,1,0:T(8,128)(2,1)}, bf16[2,128,512]{2,1,0:T(8,128)(2,1)S(1)}, u32[]{:S(2)}, u32[]{:S(2)}) collective-permute-start(bf16[2,128,512]{2,1,0:T(8,128)(2,1)} %get-tuple-element.57), channel_id=1, source_target_pairs={{0,2},{1,3},{2,0},{3,1},{4,6},{5,7},{6,4},{7,5},{8,10},{9,11},{10,... | collective-permute-start | bytes 786440 | tf_op jit(solution)/shard_map/ppermute | solution.py:437
  9.6 13.7 %collective-permute-start.12 = (bf16[2,128,512]{2,1,0:T(8,128)(2,1)S(1)}, bf16[2,128,512]{2,1,0:T(8,128)(2,1)S(1)}, u32[]{:S(2)}, u32[]{:S(2)}) collective-permute-start(bf16[2,128,512]{2,1,0:T(8,128)(2,1)S(1)} %get-tuple-element.58), channel_id=1, source_target_pairs={{0,3},{1,2},{2,1},{3,0},{4,7},{5,6},{6,5},{7,4},{8,11},{9,10},{10,... | collective-permute-start | bytes 786440 | tf_op jit(solution)/shard_map/ppermute | solution.py:437
  12.4 15.6 %collective-permute-start.13 = (bf16[512,256]{1,0:T(8,128)(2,1)S(1)}, bf16[512,256]{1,0:T(8,128)(2,1)}, u32[]{:S(2)}, u32[]{:S(2)}) collective-permute-start(bf16[512,256]{1,0:T(8,128)(2,1)S(1)} %get-tuple-element.59.refs_4_), channel_id=1, source_target_pairs={{0,4},{4,8},{8,12},{12,16},{16,20},{20,24},{24,28},{1,5},{5,9},{9,... | collective-permute-start | bytes 786440 | tf_op jit(solution)/shard_map/ppermute | solution.py:459
  16.5 0.7 copy-start
  17.2 10.8 %all-to-all-start = ((f32[8,1,512]{2,1,0:T(1,128)}), f32[8,1,512]{2,1,0:T(1,128)S(1)}, u32[]{:S(2)}, u32[]{:S(2)}) async-start(f32[8,1,512]{2,1,0:T(1,128)} %get-tuple-element.50), calls=%async_computation | async-start | bytes 32768 | tf_op jit(solution)/shard_map/all_to_all | solution.py:460
  21.4 18.0 %collective-permute-start = (bf16[2,128,512]{2,1,0:T(8,128)(2,1)S(1)}, bf16[2,128,512]{2,1,0:T(8,128)(2,1)S(1)}, u32[]{:S(2)}, u32[]{:S(2)}) collective-permute-start(bf16[2,128,512]{2,1,0:T(8,128)(2,1)S(1)} %get-tuple-element.42), channel_id=1, source_target_pairs={{0,1},{1,0},{2,3},{3,2},{4,5},{5,4},{6,7},{7,6},{8,9},{9,8},{10,11... | collective-permute-start | bytes 786440 | tf_op jit(solution)/shard_map/ppermute | solution.py:437
  21.6 17.7 %collective-permute-start.1 = (bf16[2,128,512]{2,1,0:T(8,128)(2,1)S(1)}, bf16[2,128,512]{2,1,0:T(8,128)(2,1)S(1)}, u32[]{:S(2)}, u32[]{:S(2)}) collective-permute-start(bf16[2,128,512]{2,1,0:T(8,128)(2,1)S(1)} %get-tuple-element.43), channel_id=1, source_target_pairs={{0,2},{1,3},{2,0},{3,1},{4,6},{5,7},{6,4},{7,5},{8,10},{9,11},{10,... | collective-permute-start | bytes 786440 | tf_op jit(solution)/shard_map/ppermute | solution.py:437
  23.1 16.2 %collective-permute-start.2 = (bf16[2,128,512]{2,1,0:T(8,128)(2,1)S(1)}, bf16[2,128,512]{2,1,0:T(8,128)(2,1)}, u32[]{:S(2)}, u32[]{:S(2)}) collective-permute-start(bf16[2,128,512]{2,1,0:T(8,128)(2,1)S(1)} %get-tuple-element.44), channel_id=1, source_target_pairs={{0,3},{1,2},{2,1},{3,0},{4,7},{5,6},{6,5},{7,4},{8,11},{9,10},{10,... | collective-permute-start | bytes 786440 | tf_op jit(solution)/shard_map/ppermute | solution.py:437
  23.2 16.1 %collective-permute-start.6 = (bf16[512,256]{1,0:T(8,128)(2,1)S(1)}, bf16[512,256]{1,0:T(8,128)(2,1)S(1)}, u32[]{:S(2)}, u32[]{:S(2)}) collective-permute-start(bf16[512,256]{1,0:T(8,128)(2,1)S(1)} %get-tuple-element.49.refs_4_), channel_id=1, source_target_pairs={{0,4},{4,8},{8,12},{12,16},{16,20},{20,24},{24,28},{1,5},{5,9},{9,... | collective-permute-start | bytes 786440 | tf_op jit(solution)/shard_map/ppermute | solution.py:458
  28.0 1.0 %copy-start.1 = (bf16[512,256]{1,0:T(8,128)(2,1)S(1)}, bf16[512,256]{1,0:T(8,128)(2,1)}, u32[]{:S(2)}) copy-start(bf16[512,256]{1,0:T(8,128)(2,1)} %copy-done) | copy-start | bytes 786436
  38.0 15.4 %collective-permute-start.18 = (bf16[512,256]{1,0:T(8,128)(2,1)S(1)}, bf16[512,256]{1,0:T(8,128)(2,1)S(1)}, u32[]{:S(2)}, u32[]{:S(2)}) collective-permute-start(bf16[512,256]{1,0:T(8,128)(2,1)S(1)} %get-tuple-element.69), channel_id=1, source_target_pairs={{4,0},{8,4},{12,8},{16,12},{20,16},{24,20},{28,24},{5,1},{9,5},{13... | collective-permute-start | bytes 786440 | tf_op jit(solution)/shard_map/ppermute | solution.py:465
  39.4 0.7 copy-start.2
  40.1 0.9 %copy-start.3 = (bf16[512,256]{1,0:T(8,128)(2,1)S(1)}, bf16[512,256]{1,0:T(8,128)(2,1)}, u32[]{:S(2)}) copy-start(bf16[512,256]{1,0:T(8,128)(2,1)} %copy-done.2) | copy-start | bytes 786436
  50.2 10.1 %collective-permute-start.17 = (bf16[512,256]{1,0:T(8,128)(2,1)S(1)}, bf16[512,256]{1,0:T(8,128)(2,1)S(1)}, u32[]{:S(2)}, u32[]{:S(2)}) collective-permute-start(bf16[512,256]{1,0:T(8,128)(2,1)S(1)} %get-tuple-element.68), channel_id=1, source_target_pairs={{4,0},{8,4},{12,8},{16,12},{20,16},{24,20},{28,24},{5,1},{9,5},{13... | collective-permute-start | bytes 786440 | tf_op jit(solution)/shard_map/ppermute | solution.py:463
  51.5 10.3 %collective-permute-start.14 = (bf16[2,128,512]{2,1,0:T(8,128)(2,1)S(1)}, bf16[2,128,512]{2,1,0:T(8,128)(2,1)S(1)}, u32[]{:S(2)}, u32[]{:S(2)}) collective-permute-start(bf16[2,128,512]{2,1,0:T(8,128)(2,1)S(1)} %get-tuple-element.61), channel_id=1, source_target_pairs={{0,1},{1,0},{2,3},{3,2},{4,5},{5,4},{6,7},{7,6},{8,9},{9,8},{10,11... | collective-permute-start | bytes 786440 | tf_op jit(solution)/shard_map/ppermute | solution.py:437
  51.5 10.9 %collective-permute-start.15 = (bf16[2,128,512]{2,1,0:T(8,128)(2,1)S(1)}, bf16[2,128,512]{2,1,0:T(8,128)(2,1)S(1)}, u32[]{:S(2)}, u32[]{:S(2)}) collective-permute-start(bf16[2,128,512]{2,1,0:T(8,128)(2,1)S(1)} %get-tuple-element.62), channel_id=1, source_target_pairs={{0,2},{1,3},{2,0},{3,1},{4,6},{5,7},{6,4},{7,5},{8,10},{9,11},{10,... | collective-permute-start | bytes 786440 | tf_op jit(solution)/shard_map/ppermute | solution.py:437
  53.1 12.3 %collective-permute-start.16 = (bf16[2,128,512]{2,1,0:T(8,128)(2,1)S(1)}, bf16[2,128,512]{2,1,0:T(8,128)(2,1)S(1)}, u32[]{:S(2)}, u32[]{:S(2)}) collective-permute-start(bf16[2,128,512]{2,1,0:T(8,128)(2,1)S(1)} %get-tuple-element.63), channel_id=1, source_target_pairs={{0,3},{1,2},{2,1},{3,0},{4,7},{5,6},{6,5},{7,4},{8,11},{9,10},{10,... | collective-permute-start | bytes 786440 | tf_op jit(solution)/shard_map/ppermute | solution.py:437
  53.4 13.5 %collective-permute-start.7 = (bf16[2,128,512]{2,1,0:T(8,128)(2,1)S(1)}, bf16[2,128,512]{2,1,0:T(8,128)(2,1)S(1)}, u32[]{:S(2)}, u32[]{:S(2)}) collective-permute-start(bf16[2,128,512]{2,1,0:T(8,128)(2,1)S(1)} %get-tuple-element.52), channel_id=1, source_target_pairs={{0,1},{1,0},{2,3},{3,2},{4,5},{5,4},{6,7},{7,6},{8,9},{9,8},{10,11... | collective-permute-start | bytes 786440 | tf_op jit(solution)/shard_map/ppermute | solution.py:437
  60.2 16.0 %collective-permute-start.8 = (bf16[2,128,512]{2,1,0:T(8,128)(2,1)S(1)}, bf16[2,128,512]{2,1,0:T(8,128)(2,1)S(1)}, u32[]{:S(2)}, u32[]{:S(2)}) collective-permute-start(bf16[2,128,512]{2,1,0:T(8,128)(2,1)S(1)} %get-tuple-element.53), channel_id=1, source_target_pairs={{0,2},{1,3},{2,0},{3,1},{4,6},{5,7},{6,4},{7,5},{8,10},{9,11},{10,... | collective-permute-start | bytes 786440 | tf_op jit(solution)/shard_map/ppermute | solution.py:437
  61.7 15.0 %collective-permute-start.9 = (bf16[2,128,512]{2,1,0:T(8,128)(2,1)S(1)}, bf16[2,128,512]{2,1,0:T(8,128)(2,1)S(1)}, u32[]{:S(2)}, u32[]{:S(2)}) collective-permute-start(bf16[2,128,512]{2,1,0:T(8,128)(2,1)S(1)} %get-tuple-element.54), channel_id=1, source_target_pairs={{0,3},{1,2},{2,1},{3,0},{4,7},{5,6},{6,5},{7,4},{8,11},{9,10},{10,... | collective-permute-start | bytes 786440 | tf_op jit(solution)/shard_map/ppermute | solution.py:437
  62.4 23.7 %collective-permute-start.19 = (bf16[128,512]{1,0:T(8,128)(2,1)}, bf16[128,512]{1,0:T(8,128)(2,1)S(1)}, u32[]{:S(2)}, u32[]{:S(2)}) collective-permute-start(bf16[128,512]{1,0:T(8,128)(2,1)} %get-tuple-element.71), channel_id=1, source_target_pairs={{0,1},{1,0},{2,3},{3,2},{4,5},{5,4},{6,7},{7,6},{8,9},{9,8},{10,11... | collective-permute-start | bytes 393224 | tf_op jit(solution)/shard_map/ppermute | solution.py:437
  65.4 20.7 %collective-permute-start.20 = (bf16[128,512]{1,0:T(8,128)(2,1)S(1)}, bf16[128,512]{1,0:T(8,128)(2,1)S(1)}, u32[]{:S(2)}, u32[]{:S(2)}) collective-permute-start(bf16[128,512]{1,0:T(8,128)(2,1)S(1)} %get-tuple-element.72), channel_id=1, source_target_pairs={{0,2},{1,3},{2,0},{3,1},{4,6},{5,7},{6,4},{7,5},{8,10},{9,11},{10,... | collective-permute-start | bytes 393224 | tf_op jit(solution)/shard_map/ppermute | solution.py:437
  66.8 19.3 %collective-permute-start.21 = (bf16[128,512]{1,0:T(8,128)(2,1)S(1)}, bf16[128,512]{1,0:T(8,128)(2,1)S(1)}, u32[]{:S(2)}, u32[]{:S(2)}) collective-permute-start(bf16[128,512]{1,0:T(8,128)(2,1)S(1)} %get-tuple-element.73), channel_id=1, source_target_pairs={{0,3},{1,2},{2,1},{3,0},{4,7},{5,6},{6,5},{7,4},{8,11},{9,10},{10,... | collective-permute-start | bytes 393224 | tf_op jit(solution)/shard_map/ppermute | solution.py:437
  68.2 17.9 %all-to-all-start.1 = ((f32[32,1,512]{2,1,0:T(1,128)}), f32[32,1,512]{2,1,0:T(1,128)S(1)}, u32[]{:S(2)}, u32[]{:S(2)}) async-start(f32[32,1,512]{2,1,0:T(1,128)} %spread.1), calls=%async_computation.1 | async-start | bytes 131072 | tf_op jit(solution)/shard_map/all_to_all | solution.py:468

commit v2 on v1

--- a/solution.py
+++ b/solution.py
@@ -162,21 +162,21 @@
         cuts = [0] + list(range(pad + TILE, extent(tile) + 1, TILE))
         return list(zip(cuts[:-1], cuts[1:]))
 
-    def fetch(head):
+    def fetch(head, slot):
         for d, piece in enumerate(pieces):
             at = rows_of(d, small)
-            qs[at, :] = piece[0, :, cols_of(head, DEPTH)]
-            gs[at, :] = piece[1, :, cols_of(head, DEPTH)]
+            qs[slot, at, :] = piece[0, :, cols_of(head, DEPTH)]
+            gs[slot, at, :] = piece[1, :, cols_of(head, DEPTH)]
 
     def rows_in(tile):
         return slice(tile * TILE, (tile + 1) * TILE)
 
-    def scores(tile):
+    def scores(tile, slot):
         state = dict(own=jnp.full((1, TILE), LOWEST, F32), prev=jnp.full((1, TILE), LOWEST, F32))
 
         def part(lo, hi):
             def go():
-                s = dot(kc[lo:hi], qs[rows_in(tile), :], 1, 1)
+                s = dot(kc[lo:hi], qs[slot, rows_in(tile), :], 1, 1)
                 if lo == 0:
                     at = lax.broadcasted_iota(jnp.int32, (pad, TILE), 0)
                     first = jnp.where(at < ctx, s[:pad], LOWEST)
@@ -217,7 +217,7 @@
 
         return [part(lo, hi) for lo, hi in chunks(tile)]
 
-    def gradients(tile, state):
+    def gradients(tile, state, slot):
         edge = extent(tile)
         rows = rows_in(tile)
 
@@ -225,7 +225,7 @@
             inv = 1.0 / state["total"]
             attended = dot(vt[:, :edge], lbufs[tile][:edge], 1, 0) * inv
             os[rows, :] = attended.T.astype(BF)
-            gt = (gs[rows, :].astype(F32).T * (16.0 * inv)).astype(BF)
+            gt = (gs[slot, rows, :].astype(F32).T * (16.0 * inv)).astype(BF)
             state["gt"] = gt
             state["dot"] = jnp.sum(gt.astype(F32) * attended, axis=0, keepdims=True)
 
@@ -242,7 +242,7 @@
         def store(lo, hi):
             def go():
                 dv[lo:hi] += dot(lbufs[tile][lo:hi], state["gt"], 1, 1)
-                dk[lo:hi] += dot(dbuf[lo:hi], qs[rows, :], 1, 0)
+                dk[lo:hi] += dot(dbuf[lo:hi], qs[slot, rows, :], 1, 0)
 
             return go
 
@@ -256,20 +256,20 @@
         for item in sorted(order, key=lambda x: x[:3]):
             item[3]()
 
-    fetch(0)
-    weave(scores(0))
+    fetch(0, 0)
+    weave(scores(0, 0))
 
     def step(head, carry):
         first, second = {}, {}
-        weave(scores(1), weigh(0, first))
-        weave(gradients(0, first), weigh(1, second))
-        weave(gradients(1, second))
+        slot = head % 2
+        later = jnp.minimum(head + 1, GROUP - 1)
+        weave(scores(1, slot), weigh(0, first))
+        weave(weigh(1, second), gradients(0, first, slot))
+        weave(gradients(1, second, slot), [lambda: fetch(later, 1 - slot)] + scores(0, 1 - slot))
         for d, out in enumerate(outs):
             at = rows_of(d, small)
             out[0, :, cols_of(head, DEPTH)] = os[at, :]
             out[1, :, cols_of(head, DEPTH)] = dqs[at, :]
-        fetch(jnp.minimum(head + 1, GROUP - 1))
-        weave(scores(0))
         return carry
 
     lax.fori_loop(0, GROUP, step, 0)
@@ -304,8 +304,8 @@
             pltpu.VMEM((DEPTH, width), BF),
             pltpu.VMEM((width, DEPTH), F32),
             pltpu.VMEM((width, DEPTH), F32),
-            pltpu.VMEM((BLOCK, DEPTH), BF),
-            pltpu.VMEM((BLOCK, DEPTH), BF),
+            pltpu.VMEM((2, BLOCK, DEPTH), BF),
+            pltpu.VMEM((2, BLOCK, DEPTH), BF),
             pltpu.VMEM((BLOCK, DEPTH), BF),
             pltpu.VMEM((BLOCK, DEPTH), BF),
             pltpu.VMEM((width - TILE, TILE), F32),

time: 87.6 us -> 87.4 us (level)
  no operation moved by 1% of the time
where the time goes in v2:
time: 87.4 us; the launch traced here: 86.9 us
  starting transfers between devices  36.5 us (42%)
  Pallas kernels  26.2 us (30%)
  waiting for transfers between devices  20.1 us (23%)
  local copies, waits for them, and re-layouts  3.3 us (4%)
    pallas_call x2, Pallas kernels, attend(): pl.pallas_call(lambda *refs: attend_kernel(parts, which, *refs), in_specs...  18.1 us
    ppermute x18, starting transfers between devices, swap(): moved.append(lax.ppermute(pieces[d], 'head', pairs))  13.8 us
    all_to_all x1, waiting for transfers between devices, layer(): ds = lax.all_to_all(ds, ('ctx', 'head'), 0, 0, tiled=True)  8.05 us
    all_to_all x1, starting transfers between devices, layer(): ds = lax.all_to_all(ds, ('ctx', 'head'), 0, 0, tiled=True)  7.95 us
    ppermute x1, waiting for transfers between devices, layer(): edge_a = lax.ppermute(edge_a, 'ctx', back)  6.46 us
    ppermute x18, waiting for transfers between devices, swap(): moved.append(lax.ppermute(pieces[d], 'head', pairs))  4.79 us
    all_to_all x1, starting transfers between devices, layer(): sums = lax.all_to_all(sums, 'ctx', 0, 0, tiled=True)  4.18 us
    ppermute x1, starting transfers between devices, layer(): prev_b = lax.ppermute(kv_b, 'ctx', forth)  4.12 us
  transfers between devices with their start and end apart: 24, of which 6 were waited for; matrix products, arithmetic and copies ran while one was open for 0% of the time, Pallas kernels for 28%

profile of v2, /device:TPU:0, one launch (start us, length us, event | category | flops | bytes accessed | tf_op | source)
XLA Modules:
  0.0 86.9 jit_solution(10487105614465468442)
XLA Ops:
  0.6 1.1 %pack_kv.1 = (bf16[128,512]{1,0:T(8,128)(2,1)S(1)}, bf16[128,512]{1,0:T(8,128)(2,1)S(1)}, bf16[128,512]{1,0:T(8,128)(2,1)S(1)}, bf16[128,512]{1,0:T(8,128)(2,1)S(1)}) custom-call(bf16[128,1024]{1,0:T(8,128)(2,1)} %k_ref.1, bf16[128,1024]{1,0:T(8,128)(2,1)} %v_ref.1), custom_call_target="tpu_custom_call" | custom-call | tf_op jit(solution)/shard_map/pack_kv/pallas_call | solution.py:64
  1.8 0.6 collective-permute-start.3
  2.3 2.6 %collective-permute-start.4 = (bf16[128,512]{1,0:T(8,128)(2,1)S(1)}, bf16[128,512]{1,0:T(8,128)(2,1)S(1)}, u32[]{:S(2)}, u32[]{:S(2)}) collective-permute-start(bf16[128,512]{1,0:T(8,128)(2,1)S(1)} %get-tuple-element.47), channel_id=1, source_target_pairs={{0,2},{1,3},{2,0},{3,1},{4,6},{5,7},{6,4},{7,5},{8,10},{9,11},{10,... | collective-permute-start | bytes 393224 | tf_op jit(solution)/shard_map/ppermute | solution.py:437
  4.9 0.0 collective-permute-start.5
  4.9 2.4 %pack.1 = (bf16[2,128,512]{2,1,0:T(8,128)(2,1)S(1)}, bf16[2,128,512]{2,1,0:T(8,128)(2,1)S(1)}, bf16[2,128,512]{2,1,0:T(8,128)(2,1)S(1)}, bf16[2,128,512]{2,1,0:T...) custom-call(bf16[128,4096]{1,0:T(8,128)(2,1)} %q_ref.1, ...), custom_call_target="tpu_custom_call" | custom-call | tf_op jit(solution)/shard_map/pack/pallas_call | solution.py:89
  7.4 0.2 collective-permute-start.10
  7.6 1.9 %collective-permute-start.11 = (bf16[2,128,512]{2,1,0:T(8,128)(2,1)}, bf16[2,128,512]{2,1,0:T(8,128)(2,1)S(1)}, u32[]{:S(2)}, u32[]{:S(2)}) collective-permute-start(bf16[2,128,512]{2,1,0:T(8,128)(2,1)} %get-tuple-element.57), channel_id=1, source_target_pairs={{0,2},{1,3},{2,0},{3,1},{4,6},{5,7},{6,4},{7,5},{8,10},{9,11},{10,... | collective-permute-start | bytes 786440 | tf_op jit(solution)/shard_map/ppermute | solution.py:437
  9.6 0.0 collective-permute-done.3.refs_1_
  9.6 0.0 collective-permute-start.12
  9.6 0.0 collective-permute-done.4.refs_2_
  9.6 2.0 %collective-permute-done.5.refs_3_ = bf16[128,512]{1,0:T(8,128)(2,1)S(1)} collective-permute-done((bf16[128,512]{1,0:T(8,128)(2,1)S(1)}, bf16[128,512]{1,0:T(8,128)(2,1)S(1)}, u32[]{:S(2)}, u32[]{:S(2)}) %collective-permute-start.5) | collective-permute-done | bytes 131104 | tf_op jit(solution)/shard_map/ppermute | solution.py:437
  11.6 0.8 gather_kv.1
  12.4 4.1 %collective-permute-start.13 = (bf16[512,256]{1,0:T(8,128)(2,1)S(1)}, bf16[512,256]{1,0:T(8,128)(2,1)}, u32[]{:S(2)}, u32[]{:S(2)}) collective-permute-start(bf16[512,256]{1,0:T(8,128)(2,1)S(1)} %get-tuple-element.59.refs_4_), channel_id=1, source_target_pairs={{0,4},{4,8},{8,12},{12,16},{16,20},{20,24},{24,28},{1,5},{5,9},{9,... | collective-permute-start | bytes 786440 | tf_op jit(solution)/shard_map/ppermute | solution.py:459
  16.5 0.0 copy-start
  16.5 0.7 copy-done
  17.2 4.2 %all-to-all-start = ((f32[8,1,512]{2,1,0:T(1,128)}), f32[8,1,512]{2,1,0:T(1,128)S(1)}, u32[]{:S(2)}, u32[]{:S(2)}) async-start(f32[8,1,512]{2,1,0:T(1,128)} %get-tuple-element.50), calls=%async_computation | async-start | bytes 32768 | tf_op jit(solution)/shard_map/all_to_all | solution.py:460
  21.4 0.3 collective-permute-start
  21.6 0.0 collective-permute-done.10.refs_1_
  21.6 1.5 %collective-permute-start.1 = (bf16[2,128,512]{2,1,0:T(8,128)(2,1)S(1)}, bf16[2,128,512]{2,1,0:T(8,128)(2,1)S(1)}, u32[]{:S(2)}, u32[]{:S(2)}) collective-permute-start(bf16[2,128,512]{2,1,0:T(8,128)(2,1)S(1)} %get-tuple-element.43), channel_id=1, source_target_pairs={{0,2},{1,3},{2,0},{3,1},{4,6},{5,7},{6,4},{7,5},{8,10},{9,11},{10,... | collective-permute-start | bytes 786440 | tf_op jit(solution)/shard_map/ppermute | solution.py:437
  23.1 0.0 collective-permute-done.11.refs_2_
  23.1 0.1 collective-permute-start.2
  23.2 0.0 collective-permute-done.12.refs_3_
  23.2 3.9 %collective-permute-start.6 = (bf16[512,256]{1,0:T(8,128)(2,1)S(1)}, bf16[512,256]{1,0:T(8,128)(2,1)S(1)}, u32[]{:S(2)}, u32[]{:S(2)}) collective-permute-start(bf16[512,256]{1,0:T(8,128)(2,1)S(1)} %get-tuple-element.49.refs_4_), channel_id=1, source_target_pairs={{0,4},{4,8},{8,12},{12,16},{16,20},{20,24},{24,28},{1,5},{5,9},{9,... | collective-permute-start | bytes 786440 | tf_op jit(solution)/shard_map/ppermute | solution.py:458
  27.2 0.8 all-to-all-done.refs_6_
  28.0 0.0 collective-permute-done.13.refs_5_
  28.0 0.0 copy-start.1
  28.0 0.9 %copy-done.1 = bf16[512,256]{1,0:T(8,128)(2,1)S(1)} copy-done((bf16[512,256]{1,0:T(8,128)(2,1)S(1)}, bf16[512,256]{1,0:T(8,128)(2,1)}, u32[]{:S(2)}) %copy-start.1) | copy-done | bytes 262168
  28.9 9.1 %attend.3 = (bf16[2,128,512]{2,1,0:T(8,128)(2,1)S(1)}, bf16[2,128,512]{2,1,0:T(8,128)(2,1)S(1)}, bf16[2,128,512]{2,1,0:T(8,128)(2,1)S(1)}, bf16[2,128,512]{2,1,0...) custom-call(bf16[2,128,512]{2,1,0:T(8,128)(2,1)S(1)} %get-tuple-element.55.refs_0_, ...), custom_call_target="tpu_custom_call" | custom-call | flops 3221225472 | bytes 2097152 | tf_op jit(solution)/shard_map/attend/pallas_call | solution.py:290
  38.0 1.3 %collective-permute-start.18 = (bf16[512,256]{1,0:T(8,128)(2,1)S(1)}, bf16[512,256]{1,0:T(8,128)(2,1)S(1)}, u32[]{:S(2)}, u32[]{:S(2)}) collective-permute-start(bf16[512,256]{1,0:T(8,128)(2,1)S(1)} %get-tuple-element.69), channel_id=1, source_target_pairs={{4,0},{8,4},{12,8},{16,12},{20,16},{24,20},{28,24},{5,1},{9,5},{13... | collective-permute-start | bytes 786440 | tf_op jit(solution)/shard_map/ppermute | solution.py:465
  39.3 0.0 collective-permute-done.refs_1_
  39.3 0.0 collective-permute-done.1.refs_2_
  39.3 0.0 collective-permute-done.2.refs_3_
  39.3 0.0 collective-permute-done.6.refs_5_
  39.3 0.0 copy-start.2
  39.3 0.7 copy-done.2
  40.0 0.9 %copy-done.3 = bf16[512,256]{1,0:T(8,128)(2,1)S(1)} copy-done((bf16[512,256]{1,0:T(8,128)(2,1)S(1)}, bf16[512,256]{1,0:T(8,128)(2,1)}, u32[]{:S(2)}) %copy-start.3) | copy-done | bytes 262168
  41.0 9.1 %attend.2 = (bf16[2,128,512]{2,1,0:T(8,128)(2,1)S(1)}, bf16[2,128,512]{2,1,0:T(8,128)(2,1)S(1)}, bf16[2,128,512]{2,1,0:T(8,128)(2,1)S(1)}, bf16[2,128,512]{2,1,0...) custom-call(bf16[2,128,512]{2,1,0:T(8,128)(2,1)S(1)} %get-tuple-element.41.refs_0_, ...), custom_call_target="tpu_custom_call" | custom-call | flops 3221225472 | bytes 2097152 | tf_op jit(solution)/shard_map/attend/pallas_call | solution.py:290
  50.0 1.3 %collective-permute-start.17 = (bf16[512,256]{1,0:T(8,128)(2,1)S(1)}, bf16[512,256]{1,0:T(8,128)(2,1)S(1)}, u32[]{:S(2)}, u32[]{:S(2)}) collective-permute-start(bf16[512,256]{1,0:T(8,128)(2,1)S(1)} %get-tuple-element.68), channel_id=1, source_target_pairs={{4,0},{8,4},{12,8},{16,12},{20,16},{24,20},{28,24},{5,1},{9,5},{13... | collective-permute-start | bytes 786440 | tf_op jit(solution)/shard_map/ppermute | solution.py:463
  51.3 0.1 collective-permute-start.14
  51.4 1.5 %collective-permute-start.15 = (bf16[2,128,512]{2,1,0:T(8,128)(2,1)S(1)}, bf16[2,128,512]{2,1,0:T(8,128)(2,1)S(1)}, u32[]{:S(2)}, u32[]{:S(2)}) collective-permute-start(bf16[2,128,512]{2,1,0:T(8,128)(2,1)S(1)} %get-tuple-element.62), channel_id=1, source_target_pairs={{0,2},{1,3},{2,0},{3,1},{4,6},{5,7},{6,4},{7,5},{8,10},{9,11},{10,... | collective-permute-start | bytes 786440 | tf_op jit(solution)/shard_map/ppermute | solution.py:437
  52.9 0.3 collective-permute-start.16
  53.3 0.0 collective-permute-done.18.edge_b
  53.3 0.4 collective-permute-start.7
  53.6 6.5 %collective-permute-done.17.edge_a = bf16[512,256]{1,0:T(8,128)(2,1)S(1)} collective-permute-done((bf16[512,256]{1,0:T(8,128)(2,1)S(1)}, bf16[512,256]{1,0:T(8,128)(2,1)S(1)}, u32[]{:S(2)}, u32[]{:S(2)}) %collective-permute-start.17) | collective-permute-done | bytes 262176 | tf_op jit(solution)/shard_map/ppermute | solution.py:463
  60.1 1.5 %collective-permute-start.8 = (bf16[2,128,512]{2,1,0:T(8,128)(2,1)S(1)}, bf16[2,128,512]{2,1,0:T(8,128)(2,1)S(1)}, u32[]{:S(2)}, u32[]{:S(2)}) collective-permute-start(bf16[2,128,512]{2,1,0:T(8,128)(2,1)S(1)} %get-tuple-element.53), channel_id=1, source_target_pairs={{0,2},{1,3},{2,0},{3,1},{4,6},{5,7},{6,4},{7,5},{8,10},{9,11},{10,... | collective-permute-start | bytes 786440 | tf_op jit(solution)/shard_map/ppermute | solution.py:437
  61.6 0.0 collective-permute-done.14.refs_5_
  61.6 0.0 collective-permute-start.9
  61.6 0.7 join.1
  62.3 0.0 collective-permute-done.15.refs_6_
  62.3 0.7 collective-permute-start.19
  62.9 2.3 %collective-permute-done.16.refs_7_ = bf16[2,128,512]{2,1,0:T(8,128)(2,1)S(1)} collective-permute-done((bf16[2,128,512]{2,1,0:T(8,128)(2,1)S(1)}, bf16[2,128,512]{2,1,0:T(8,128)(2,1)S(1)}, u32[]{:S(2)}, u32[]{:S(2)}) %collective-permute-start.16) | collective-permute-done | bytes 262176 | tf_op jit(solution)/shard_map/ppermute | solution.py:437
  65.3 1.4 %collective-permute-start.20 = (bf16[128,512]{1,0:T(8,128)(2,1)S(1)}, bf16[128,512]{1,0:T(8,128)(2,1)S(1)}, u32[]{:S(2)}, u32[]{:S(2)}) collective-permute-start(bf16[128,512]{1,0:T(8,128)(2,1)S(1)} %get-tuple-element.72), channel_id=1, source_target_pairs={{0,2},{1,3},{2,0},{3,1},{4,6},{5,7},{6,4},{7,5},{8,10},{9,11},{10,... | collective-permute-start | bytes 393224 | tf_op jit(solution)/shard_map/ppermute | solution.py:437
  66.7 0.0 collective-permute-done.7.refs_1_
  66.7 0.8 collective-permute-start.21
  67.4 0.7 spread.1
  68.1 7.9 %all-to-all-start.1 = ((f32[32,1,512]{2,1,0:T(1,128)}), f32[32,1,512]{2,1,0:T(1,128)S(1)}, u32[]{:S(2)}, u32[]{:S(2)}) async-start(f32[32,1,512]{2,1,0:T(1,128)} %spread.1), calls=%async_computation.1 | async-start | bytes 131072 | tf_op jit(solution)/shard_map/all_to_all | solution.py:468
  76.1 0.0 collective-permute-done.8.refs_2_
  76.1 0.4 collective-permute-done.9.refs_3_
  76.5 1.4 %unpack.1 = (bf16[128,4096]{1,0:T(8,128)(2,1)}, bf16[128,4096]{1,0:T(8,128)(2,1)}) custom-call(bf16[2,128,512]{2,1,0:T(8,128)(2,1)S(1)} %get-tuple-element.51.refs_0_, bf16[2,128,512]{2,1,0:T(8,128)(2,1)S(1)} %collective-permute-done.7.refs_1_, bf16[2,128,512]{2,1,0:T(8,128)(2,1)S(1)} %collective-permute-done.8.refs_2_, ...), custom_call_target="tpu_custom_call" | custom-call | tf_op jit(solution)/shard_map/unpack/pallas_call | solution.py:391
  77.9 8.0 %all-to-all-done.1.refs_4_ = f32[32,1,512]{2,1,0:T(1,128)S(1)} async-done(((f32[32,1,512]{2,1,0:T(1,128)}), f32[32,1,512]{2,1,0:T(1,128)S(1)}, u32[]{:S(2)}, u32[]{:S(2)}) %all-to-all-start.1) | async-done | bytes 65568 | tf_op jit(solution)/shard_map/all_to_all | solution.py:468
  86.0 0.0 collective-permute-done.19.refs_1_
  86.0 0.0 collective-permute-done.20.refs_2_
  86.0 0.0 collective-permute-done.21.refs_3_
  86.0 0.9 %finish.1 = (bf16[128,1024]{1,0:T(8,128)(2,1)}, bf16[128,1024]{1,0:T(8,128)(2,1)}) custom-call(bf16[128,512]{1,0:T(8,128)(2,1)S(1)} %get-tuple-element.70.refs_0_, bf16[128,512]{1,0:T(8,128)(2,1)S(1)} %collective-permute-done.19.refs_1_, bf16[128,512]{1,0:T(8,128)(2,1)S(1)} %collective-permute-done.20.refs_2_, ...), custom_call_target="tpu_custom_call" | custom-call | tf_op jit(solution)/shard_map/finish/pallas_call | solution.py:421
  (1 shorter events, 0.0 us)
Async XLA Ops:
  1.8 7.8 %collective-permute-start.3 = (bf16[128,512]{1,0:T(8,128)(2,1)S(1)}, bf16[128,512]{1,0:T(8,128)(2,1)S(1)}, u32[]{:S(2)}, u32[]{:S(2)}) collective-permute-start(bf16[128,512]{1,0:T(8,128)(2,1)S(1)} %get-tuple-element.46), channel_id=1, source_target_pairs={{0,1},{1,0},{2,3},{3,2},{4,5},{5,4},{6,7},{7,6},{8,9},{9,8},{10,11... | collective-permute-start | bytes 393224 | tf_op jit(solution)/shard_map/ppermute | solution.py:437
  2.3 7.2 %collective-permute-start.4 = (bf16[128,512]{1,0:T(8,128)(2,1)S(1)}, bf16[128,512]{1,0:T(8,128)(2,1)S(1)}, u32[]{:S(2)}, u32[]{:S(2)}) collective-permute-start(bf16[128,512]{1,0:T(8,128)(2,1)S(1)} %get-tuple-element.47), channel_id=1, source_target_pairs={{0,2},{1,3},{2,0},{3,1},{4,6},{5,7},{6,4},{7,5},{8,10},{9,11},{10,... | collective-permute-start | bytes 393224 | tf_op jit(solution)/shard_map/ppermute | solution.py:437
  4.9 6.7 %collective-permute-start.5 = (bf16[128,512]{1,0:T(8,128)(2,1)S(1)}, bf16[128,512]{1,0:T(8,128)(2,1)S(1)}, u32[]{:S(2)}, u32[]{:S(2)}) collective-permute-start(bf16[128,512]{1,0:T(8,128)(2,1)S(1)} %get-tuple-element.48), channel_id=1, source_target_pairs={{0,3},{1,2},{2,1},{3,0},{4,7},{5,6},{6,5},{7,4},{8,11},{9,10},{10,... | collective-permute-start | bytes 393224 | tf_op jit(solution)/shard_map/ppermute | solution.py:437
  7.4 14.2 %collective-permute-start.10 = (bf16[2,128,512]{2,1,0:T(8,128)(2,1)S(1)}, bf16[2,128,512]{2,1,0:T(8,128)(2,1)S(1)}, u32[]{:S(2)}, u32[]{:S(2)}) collective-permute-start(bf16[2,128,512]{2,1,0:T(8,128)(2,1)S(1)} %get-tuple-element.56), channel_id=1, source_target_pairs={{0,1},{1,0},{2,3},{3,2},{4,5},{5,4},{6,7},{7,6},{8,9},{9,8},{10,11... | collective-permute-start | bytes 786440 | tf_op jit(solution)/shard_map/ppermute | solution.py:437
  7.6 15.5 %collective-permute-start.11 = (bf16[2,128,512]{2,1,0:T(8,128)(2,1)}, bf16[2,128,512]{2,1,0:T(8,128)(2,1)S(1)}, u32[]{:S(2)}, u32[]{:S(2)}) collective-permute-start(bf16[2,128,512]{2,1,0:T(8,128)(2,1)} %get-tuple-element.57), channel_id=1, source_target_pairs={{0,2},{1,3},{2,0},{3,1},{4,6},{5,7},{6,4},{7,5},{8,10},{9,11},{10,... | collective-permute-start | bytes 786440 | tf_op jit(solution)/shard_map/ppermute | solution.py:437
  9.6 13.7 %collective-permute-start.12 = (bf16[2,128,512]{2,1,0:T(8,128)(2,1)S(1)}, bf16[2,128,512]{2,1,0:T(8,128)(2,1)S(1)}, u32[]{:S(2)}, u32[]{:S(2)}) collective-permute-start(bf16[2,128,512]{2,1,0:T(8,128)(2,1)S(1)} %get-tuple-element.58), channel_id=1, source_target_pairs={{0,3},{1,2},{2,1},{3,0},{4,7},{5,6},{6,5},{7,4},{8,11},{9,10},{10,... | collective-permute-start | bytes 786440 | tf_op jit(solution)/shard_map/ppermute | solution.py:437
  12.4 15.6 %collective-permute-start.13 = (bf16[512,256]{1,0:T(8,128)(2,1)S(1)}, bf16[512,256]{1,0:T(8,128)(2,1)}, u32[]{:S(2)}, u32[]{:S(2)}) collective-permute-start(bf16[512,256]{1,0:T(8,128)(2,1)S(1)} %get-tuple-element.59.refs_4_), channel_id=1, source_target_pairs={{0,4},{4,8},{8,12},{12,16},{16,20},{20,24},{24,28},{1,5},{5,9},{9,... | collective-permute-start | bytes 786440 | tf_op jit(solution)/shard_map/ppermute | solution.py:459
  16.5 0.7 copy-start
  17.2 10.8 %all-to-all-start = ((f32[8,1,512]{2,1,0:T(1,128)}), f32[8,1,512]{2,1,0:T(1,128)S(1)}, u32[]{:S(2)}, u32[]{:S(2)}) async-start(f32[8,1,512]{2,1,0:T(1,128)} %get-tuple-element.50), calls=%async_computation | async-start | bytes 32768 | tf_op jit(solution)/shard_map/all_to_all | solution.py:460
  21.4 17.9 %collective-permute-start = (bf16[2,128,512]{2,1,0:T(8,128)(2,1)S(1)}, bf16[2,128,512]{2,1,0:T(8,128)(2,1)S(1)}, u32[]{:S(2)}, u32[]{:S(2)}) collective-permute-start(bf16[2,128,512]{2,1,0:T(8,128)(2,1)S(1)} %get-tuple-element.42), channel_id=1, source_target_pairs={{0,1},{1,0},{2,3},{3,2},{4,5},{5,4},{6,7},{7,6},{8,9},{9,8},{10,11... | collective-permute-start | bytes 786440 | tf_op jit(solution)/shard_map/ppermute | solution.py:437
  21.6 17.6 %collective-permute-start.1 = (bf16[2,128,512]{2,1,0:T(8,128)(2,1)S(1)}, bf16[2,128,512]{2,1,0:T(8,128)(2,1)S(1)}, u32[]{:S(2)}, u32[]{:S(2)}) collective-permute-start(bf16[2,128,512]{2,1,0:T(8,128)(2,1)S(1)} %get-tuple-element.43), channel_id=1, source_target_pairs={{0,2},{1,3},{2,0},{3,1},{4,6},{5,7},{6,4},{7,5},{8,10},{9,11},{10,... | collective-permute-start | bytes 786440 | tf_op jit(solution)/shard_map/ppermute | solution.py:437
  23.1 16.2 %collective-permute-start.2 = (bf16[2,128,512]{2,1,0:T(8,128)(2,1)S(1)}, bf16[2,128,512]{2,1,0:T(8,128)(2,1)}, u32[]{:S(2)}, u32[]{:S(2)}) collective-permute-start(bf16[2,128,512]{2,1,0:T(8,128)(2,1)S(1)} %get-tuple-element.44), channel_id=1, source_target_pairs={{0,3},{1,2},{2,1},{3,0},{4,7},{5,6},{6,5},{7,4},{8,11},{9,10},{10,... | collective-permute-start | bytes 786440 | tf_op jit(solution)/shard_map/ppermute | solution.py:437
  23.2 16.1 %collective-permute-start.6 = (bf16[512,256]{1,0:T(8,128)(2,1)S(1)}, bf16[512,256]{1,0:T(8,128)(2,1)S(1)}, u32[]{:S(2)}, u32[]{:S(2)}) collective-permute-start(bf16[512,256]{1,0:T(8,128)(2,1)S(1)} %get-tuple-element.49.refs_4_), channel_id=1, source_target_pairs={{0,4},{4,8},{8,12},{12,16},{16,20},{20,24},{24,28},{1,5},{5,9},{9,... | collective-permute-start | bytes 786440 | tf_op jit(solution)/shard_map/ppermute | solution.py:458
  28.0 1.0 %copy-start.1 = (bf16[512,256]{1,0:T(8,128)(2,1)S(1)}, bf16[512,256]{1,0:T(8,128)(2,1)}, u32[]{:S(2)}) copy-start(bf16[512,256]{1,0:T(8,128)(2,1)} %copy-done) | copy-start | bytes 786436
  38.0 15.3 %collective-permute-start.18 = (bf16[512,256]{1,0:T(8,128)(2,1)S(1)}, bf16[512,256]{1,0:T(8,128)(2,1)S(1)}, u32[]{:S(2)}, u32[]{:S(2)}) collective-permute-start(bf16[512,256]{1,0:T(8,128)(2,1)S(1)} %get-tuple-element.69), channel_id=1, source_target_pairs={{4,0},{8,4},{12,8},{16,12},{20,16},{24,20},{28,24},{5,1},{9,5},{13... | collective-permute-start | bytes 786440 | tf_op jit(solution)/shard_map/ppermute | solution.py:465
  39.3 0.7 copy-start.2
  40.0 0.9 %copy-start.3 = (bf16[512,256]{1,0:T(8,128)(2,1)S(1)}, bf16[512,256]{1,0:T(8,128)(2,1)}, u32[]{:S(2)}) copy-start(bf16[512,256]{1,0:T(8,128)(2,1)} %copy-done.2) | copy-start | bytes 786436
  50.0 10.1 %collective-permute-start.17 = (bf16[512,256]{1,0:T(8,128)(2,1)S(1)}, bf16[512,256]{1,0:T(8,128)(2,1)S(1)}, u32[]{:S(2)}, u32[]{:S(2)}) collective-permute-start(bf16[512,256]{1,0:T(8,128)(2,1)S(1)} %get-tuple-element.68), channel_id=1, source_target_pairs={{4,0},{8,4},{12,8},{16,12},{20,16},{24,20},{28,24},{5,1},{9,5},{13... | collective-permute-start | bytes 786440 | tf_op jit(solution)/shard_map/ppermute | solution.py:463
  51.3 10.2 %collective-permute-start.14 = (bf16[2,128,512]{2,1,0:T(8,128)(2,1)S(1)}, bf16[2,128,512]{2,1,0:T(8,128)(2,1)S(1)}, u32[]{:S(2)}, u32[]{:S(2)}) collective-permute-start(bf16[2,128,512]{2,1,0:T(8,128)(2,1)S(1)} %get-tuple-element.61), channel_id=1, source_target_pairs={{0,1},{1,0},{2,3},{3,2},{4,5},{5,4},{6,7},{7,6},{8,9},{9,8},{10,11... | collective-permute-start | bytes 786440 | tf_op jit(solution)/shard_map/ppermute | solution.py:437
  51.4 10.9 %collective-permute-start.15 = (bf16[2,128,512]{2,1,0:T(8,128)(2,1)S(1)}, bf16[2,128,512]{2,1,0:T(8,128)(2,1)S(1)}, u32[]{:S(2)}, u32[]{:S(2)}) collective-permute-start(bf16[2,128,512]{2,1,0:T(8,128)(2,1)S(1)} %get-tuple-element.62), channel_id=1, source_target_pairs={{0,2},{1,3},{2,0},{3,1},{4,6},{5,7},{6,4},{7,5},{8,10},{9,11},{10,... | collective-permute-start | bytes 786440 | tf_op jit(solution)/shard_map/ppermute | solution.py:437
  52.9 12.3 %collective-permute-start.16 = (bf16[2,128,512]{2,1,0:T(8,128)(2,1)S(1)}, bf16[2,128,512]{2,1,0:T(8,128)(2,1)S(1)}, u32[]{:S(2)}, u32[]{:S(2)}) collective-permute-start(bf16[2,128,512]{2,1,0:T(8,128)(2,1)S(1)} %get-tuple-element.63), channel_id=1, source_target_pairs={{0,3},{1,2},{2,1},{3,0},{4,7},{5,6},{6,5},{7,4},{8,11},{9,10},{10,... | collective-permute-start | bytes 786440 | tf_op jit(solution)/shard_map/ppermute | solution.py:437
  53.3 13.4 %collective-permute-start.7 = (bf16[2,128,512]{2,1,0:T(8,128)(2,1)S(1)}, bf16[2,128,512]{2,1,0:T(8,128)(2,1)S(1)}, u32[]{:S(2)}, u32[]{:S(2)}) collective-permute-start(bf16[2,128,512]{2,1,0:T(8,128)(2,1)S(1)} %get-tuple-element.52), channel_id=1, source_target_pairs={{0,1},{1,0},{2,3},{3,2},{4,5},{5,4},{6,7},{7,6},{8,9},{9,8},{10,11... | collective-permute-start | bytes 786440 | tf_op jit(solution)/shard_map/ppermute | solution.py:437
  60.1 16.0 %collective-permute-start.8 = (bf16[2,128,512]{2,1,0:T(8,128)(2,1)S(1)}, bf16[2,128,512]{2,1,0:T(8,128)(2,1)S(1)}, u32[]{:S(2)}, u32[]{:S(2)}) collective-permute-start(bf16[2,128,512]{2,1,0:T(8,128)(2,1)S(1)} %get-tuple-element.53), channel_id=1, source_target_pairs={{0,2},{1,3},{2,0},{3,1},{4,6},{5,7},{6,4},{7,5},{8,10},{9,11},{10,... | collective-permute-start | bytes 786440 | tf_op jit(solution)/shard_map/ppermute | solution.py:437
  61.6 14.9 %collective-permute-start.9 = (bf16[2,128,512]{2,1,0:T(8,128)(2,1)S(1)}, bf16[2,128,512]{2,1,0:T(8,128)(2,1)S(1)}, u32[]{:S(2)}, u32[]{:S(2)}) collective-permute-start(bf16[2,128,512]{2,1,0:T(8,128)(2,1)S(1)} %get-tuple-element.54), channel_id=1, source_target_pairs={{0,3},{1,2},{2,1},{3,0},{4,7},{5,6},{6,5},{7,4},{8,11},{9,10},{10,... | collective-permute-start | bytes 786440 | tf_op jit(solution)/shard_map/ppermute | solution.py:437
  62.3 23.7 %collective-permute-start.19 = (bf16[128,512]{1,0:T(8,128)(2,1)}, bf16[128,512]{1,0:T(8,128)(2,1)S(1)}, u32[]{:S(2)}, u32[]{:S(2)}) collective-permute-start(bf16[128,512]{1,0:T(8,128)(2,1)} %get-tuple-element.71), channel_id=1, source_target_pairs={{0,1},{1,0},{2,3},{3,2},{4,5},{5,4},{6,7},{7,6},{8,9},{9,8},{10,11... | collective-permute-start | bytes 393224 | tf_op jit(solution)/shard_map/ppermute | solution.py:437
  65.3 20.7 %collective-permute-start.20 = (bf16[128,512]{1,0:T(8,128)(2,1)S(1)}, bf16[128,512]{1,0:T(8,128)(2,1)S(1)}, u32[]{:S(2)}, u32[]{:S(2)}) collective-permute-start(bf16[128,512]{1,0:T(8,128)(2,1)S(1)} %get-tuple-element.72), channel_id=1, source_target_pairs={{0,2},{1,3},{2,0},{3,1},{4,6},{5,7},{6,4},{7,5},{8,10},{9,11},{10,... | collective-permute-start | bytes 393224 | tf_op jit(solution)/shard_map/ppermute | solution.py:437
  66.7 19.3 %collective-permute-start.21 = (bf16[128,512]{1,0:T(8,128)(2,1)S(1)}, bf16[128,512]{1,0:T(8,128)(2,1)S(1)}, u32[]{:S(2)}, u32[]{:S(2)}) collective-permute-start(bf16[128,512]{1,0:T(8,128)(2,1)S(1)} %get-tuple-element.73), channel_id=1, source_target_pairs={{0,3},{1,2},{2,1},{3,0},{4,7},{5,6},{6,5},{7,4},{8,11},{9,10},{10,... | collective-permute-start | bytes 393224 | tf_op jit(solution)/shard_map/ppermute | solution.py:437
  68.1 17.9 %all-to-all-start.1 = ((f32[32,1,512]{2,1,0:T(1,128)}), f32[32,1,512]{2,1,0:T(1,128)S(1)}, u32[]{:S(2)}, u32[]{:S(2)}) async-start(f32[32,1,512]{2,1,0:T(1,128)} %spread.1), calls=%async_computation.1 | async-start | bytes 131072 | tf_op jit(solution)/shard_map/all_to_all | solution.py:468

commit v3 on v2

--- a/solution.py
+++ b/solution.py
@@ -241,12 +241,16 @@
 
         def store(lo, hi):
             def go():
-                dv[lo:hi] += dot(lbufs[tile][lo:hi], state["gt"], 1, 1)
                 dk[lo:hi] += dot(dbuf[lo:hi], qs[slot, rows, :], 1, 0)
 
             return go
 
         steps = [out] + [part(lo, hi) for lo, hi in chunks(tile)] + [query]
+
+        def values():
+            dv[:edge] += dot(lbufs[tile][:edge], state["gt"], 1, 1)
+
+        steps.insert(1, values)
         return steps + [store(lo, hi) for lo, hi in chunks(tile)]
 
     def weave(*stages):
@@ -277,8 +281,8 @@
     ds_ref[:, DEPTH:] = dv[:count]
     edge_ref[:, :DEPTH] = (dk[pad : pad + BLOCK] * scale).astype(BF)
     edge_ref[:, DEPTH:] = dv[pad : pad + BLOCK].astype(BF)
-    own_ref[:, :DEPTH] = dk[pad + BLOCK :] * scale
-    own_ref[:, DEPTH:] = dv[pad + BLOCK :]
+    own_ref[:, :DEPTH] = (dk[pad + BLOCK :] * scale).astype(BF)
+    own_ref[:, DEPTH:] = dv[pad + BLOCK :].astype(BF)
 
 
 def attend(pieces, kv, prev, sums, which):
@@ -294,7 +298,7 @@
         out_shape=[jax.ShapeDtypeStruct((2, small, GROUP * DEPTH), BF)] * parts
         + [
             jax.ShapeDtypeStruct((BLOCK, 2 * DEPTH), BF),
-            jax.ShapeDtypeStruct((BLOCK, 2 * DEPTH), F32),
+            jax.ShapeDtypeStruct((BLOCK, 2 * DEPTH), BF),
             jax.ShapeDtypeStruct((count, 2 * DEPTH), F32),
         ],
         scratch_shapes=[
@@ -326,25 +330,22 @@
     return outs[:parts], outs[parts], outs[parts + 1], outs[parts + 2]
 
 
-def join_kernel(own_a, own_b, edge_a, edge_b, *outs):
+def join_kernel(own, edge, *outs):
     rows = outs[0].shape[0]
     for d, out in enumerate(outs):
         at = rows_of(d, rows)
-        for g, (own, edge) in enumerate(((own_a, edge_a), (own_b, edge_b))):
-            both = (own[at, :] + edge[at, :].astype(F32)).astype(BF)
-            out[:, g * DEPTH : (g + 1) * DEPTH] = both[:, :DEPTH]
-            out[:, (2 + g) * DEPTH : (3 + g) * DEPTH] = both[:, DEPTH:]
+        out[...] = (own[at, :].astype(F32) + edge[at, :].astype(F32)).astype(BF)
 
 
 def join(own, edge, parts):
     return pl.pallas_call(
         join_kernel,
-        in_specs=[VM] * 4,
+        in_specs=[VM] * 2,
         out_specs=[VM] * parts,
-        out_shape=[jax.ShapeDtypeStruct((BLOCK // parts, 4 * DEPTH), BF)] * parts,
+        out_shape=[jax.ShapeDtypeStruct((BLOCK // parts, 2 * DEPTH), BF)] * parts,
         compiler_params=ROOM,
         name="join",
-    )(own[0], own[1], edge[0], edge[1])
+    )(own, edge)
 
 
 def spread_kernel(a_ref, b_ref, out_ref):
@@ -402,31 +403,33 @@
 def finish_kernel(*refs):
     ds_ref, dk_out, dv_out, dk_ref, dv_ref, sems = refs[-6:]
     pieces = refs[:-6]
-    parts = len(pieces)
-    wide = 2 * DEPTH
-    for d, piece in enumerate(pieces):
+    parts = len(pieces) // 2
+    for d in range(parts):
         total = sum(ds_ref[c * parts + here(d)] for c in range(ds_ref.shape[0] // parts))
-        full = (piece[...].astype(F32) + total * (1.0 / BLOCK)).astype(BF)
-        cols = cols_of(here(d), wide)
-        dk_ref[:, cols] = full[:, :wide]
-        dv_ref[:, cols] = full[:, wide:]
+        total = total * (1.0 / BLOCK)
+        for g in range(2):
+            piece = pieces[g * parts + d]
+            cols = cols_of(2 * here(d) + g, DEPTH)
+            for i, ref in enumerate((dk_ref, dv_ref)):
+                spread = total[:, (2 * i + g) * DEPTH : (2 * i + g + 1) * DEPTH]
+                half = piece[:, i * DEPTH : (i + 1) * DEPTH].astype(F32)
+                ref[:, cols] = (half + spread).astype(BF)
     pairs = ((dk_ref, dk_out), (dv_ref, dv_out))
     run([pltpu.make_async_copy(a, b, sems.at[i]) for i, (a, b) in enumerate(pairs)])
 
 
-def finish(pieces, ds):
-    parts = len(pieces)
-    rows = pieces[0].shape[0]
-    shape = (rows, parts * 2 * DEPTH)
+def finish(a, b, ds):
+    parts = len(a)
+    shape = (a[0].shape[0], parts * 2 * DEPTH)
     return pl.pallas_call(
         finish_kernel,
-        in_specs=[VM] * (parts + 1),
+        in_specs=[VM] * (2 * parts + 1),
         out_specs=[HB] * 2,
         out_shape=[jax.ShapeDtypeStruct(shape, BF)] * 2,
         scratch_shapes=[pltpu.VMEM(shape, BF)] * 2 + [pltpu.SemaphoreType.DMA((2,))],
         compiler_params=ROOM,
         name="finish",
-    )(*pieces, ds)
+    )(*a, *b, ds)
 
 
 def swap(pieces):
@@ -466,10 +469,12 @@
     out_b = swap(out_b)
     ds = spread(ds_a, ds_b, parts)
     ds = lax.all_to_all(ds, ("ctx", "head"), 0, 0, tiled=True)
-    dkv = join((own_a, own_b), (edge_a, edge_b), parts)
-    dkv = swap(dkv)
+    dkv_a = join(own_a, edge_a, parts)
+    dkv_a = swap(dkv_a)
+    dkv_b = join(own_b, edge_b, parts)
+    dkv_b = swap(dkv_b)
     out, grad_queries = unpack(out_a, out_b)
-    grad_keys, grad_values = finish(dkv, ds)
+    grad_keys, grad_values = finish(dkv_a, dkv_b, ds)
     return out, grad_queries, grad_keys, grad_values
 
 

time: 87.4 us -> 84.8 us (0.970)
  the two profiles are of different devices: /device:TPU:0 before, /device:TPU:9 now
where the time goes in v3:
time: 84.8 us; the launch traced here: 84.3 us
  starting transfers between devices  40.2 us (47%)
  Pallas kernels  26.6 us (31%)
  waiting for transfers between devices  15 us (18%)
  local copies, waits for them, and re-layouts  1.64 us (2%)
    ppermute x21, starting transfers between devices, swap(): moved.append(lax.ppermute(pieces[d], 'head', pairs))  18.4 us
    pallas_call x2, Pallas kernels, attend(): pl.pallas_call(lambda *refs: attend_kernel(parts, which, *refs), in_specs...  17.8 us
    ppermute x21, waiting for transfers between devices, swap(): moved.append(lax.ppermute(pieces[d], 'head', pairs))  11.9 us
    all_to_all x1, starting transfers between devices, layer(): ds = lax.all_to_all(ds, ('ctx', 'head'), 0, 0, tiled=True)  4.84 us
    all_to_all x1, starting transfers between devices, layer(): sums = lax.all_to_all(sums, 'ctx', 0, 0, tiled=True)  4.76 us
    ppermute x1, waiting for transfers between devices, layer(): edge_a = lax.ppermute(edge_a, 'ctx', back)  3.14 us
    ppermute x1, starting transfers between devices, layer(): prev_b = lax.ppermute(kv_b, 'ctx', forth)  3.14 us
    ppermute x1, starting transfers between devices, layer(): edge_b = lax.ppermute(edge_b, 'ctx', back)  3.09 us
  transfers between devices with their start and end apart: 27, of which 6 were waited for; matrix products, arithmetic and copies ran while one was open for 0% of the time, Pallas kernels for 29%

profile of v3, /device:TPU:9, one launch (start us, length us, event | category | flops | bytes accessed | tf_op | source)
XLA Modules:
  0.0 84.3 jit_solution(7425386855876588785)
XLA Ops:
  0.6 1.1 %pack_kv.1 = (bf16[128,512]{1,0:T(8,128)(2,1)S(1)}, bf16[128,512]{1,0:T(8,128)(2,1)S(1)}, bf16[128,512]{1,0:T(8,128)(2,1)S(1)}, bf16[128,512]{1,0:T(8,128)(2,1)S(1)}) custom-call(bf16[128,1024]{1,0:T(8,128)(2,1)} %k_ref.1, bf16[128,1024]{1,0:T(8,128)(2,1)} %v_ref.1), custom_call_target="tpu_custom_call" | custom-call | tf_op jit(solution)/shard_map/pack_kv/pallas_call | solution.py:64
  1.8 0.7 collective-permute-start.3
  2.5 1.2 %collective-permute-start.4 = (bf16[128,512]{1,0:T(8,128)(2,1)S(1)}, bf16[128,512]{1,0:T(8,128)(2,1)S(1)}, u32[]{:S(2)}, u32[]{:S(2)}) collective-permute-start(bf16[128,512]{1,0:T(8,128)(2,1)S(1)} %get-tuple-element.51), channel_id=1, source_target_pairs={{0,2},{1,3},{2,0},{3,1},{4,6},{5,7},{6,4},{7,5},{8,10},{9,11},{10,... | collective-permute-start | bytes 393224 | tf_op jit(solution)/shard_map/ppermute | solution.py:440
  3.7 0.5 collective-permute-start.5
  4.2 2.5 %pack.1 = (bf16[2,128,512]{2,1,0:T(8,128)(2,1)S(1)}, bf16[2,128,512]{2,1,0:T(8,128)(2,1)S(1)}, bf16[2,128,512]{2,1,0:T(8,128)(2,1)S(1)}, bf16[2,128,512]{2,1,0:T...) custom-call(bf16[128,4096]{1,0:T(8,128)(2,1)} %q_ref.1, ...), custom_call_target="tpu_custom_call" | custom-call | tf_op jit(solution)/shard_map/pack/pallas_call | solution.py:89
  6.8 0.2 collective-permute-start.10
  7.0 1.2 %collective-permute-start.11 = (bf16[2,128,512]{2,1,0:T(8,128)(2,1)}, bf16[2,128,512]{2,1,0:T(8,128)(2,1)S(1)}, u32[]{:S(2)}, u32[]{:S(2)}) collective-permute-start(bf16[2,128,512]{2,1,0:T(8,128)(2,1)} %get-tuple-element.61), channel_id=1, source_target_pairs={{0,2},{1,3},{2,0},{3,1},{4,6},{5,7},{6,4},{7,5},{8,10},{9,11},{10,... | collective-permute-start | bytes 786440 | tf_op jit(solution)/shard_map/ppermute | solution.py:440
  8.2 0.0 collective-permute-done.3.refs_1_
  8.2 0.8 collective-permute-start.12
  9.0 0.0 collective-permute-done.4.refs_2_
  9.0 2.1 %collective-permute-done.5.refs_3_ = bf16[128,512]{1,0:T(8,128)(2,1)S(1)} collective-permute-done((bf16[128,512]{1,0:T(8,128)(2,1)S(1)}, bf16[128,512]{1,0:T(8,128)(2,1)S(1)}, u32[]{:S(2)}, u32[]{:S(2)}) %collective-permute-start.5) | collective-permute-done | bytes 131104 | tf_op jit(solution)/shard_map/ppermute | solution.py:440
  11.1 0.8 gather_kv.1
  11.9 3.1 %collective-permute-start.13 = (bf16[512,256]{1,0:T(8,128)(2,1)S(1)}, bf16[512,256]{1,0:T(8,128)(2,1)}, u32[]{:S(2)}, u32[]{:S(2)}) collective-permute-start(bf16[512,256]{1,0:T(8,128)(2,1)S(1)} %get-tuple-element.63.refs_4_), channel_id=1, source_target_pairs={{0,4},{4,8},{8,12},{12,16},{16,20},{20,24},{24,28},{1,5},{5,9},{9,... | collective-permute-start | bytes 786440 | tf_op jit(solution)/shard_map/ppermute | solution.py:462
  15.0 0.0 copy-start
  15.0 0.7 copy-done
  15.7 4.8 %all-to-all-start = ((f32[8,1,512]{2,1,0:T(1,128)}), f32[8,1,512]{2,1,0:T(1,128)S(1)}, u32[]{:S(2)}, u32[]{:S(2)}) async-start(f32[8,1,512]{2,1,0:T(1,128)} %get-tuple-element.54), calls=%async_computation | async-start | bytes 32768 | tf_op jit(solution)/shard_map/all_to_all | solution.py:463
  20.5 0.5 collective-permute-start
  21.0 0.0 collective-permute-done.10.refs_1_
  21.0 1.1 %collective-permute-start.1 = (bf16[2,128,512]{2,1,0:T(8,128)(2,1)S(1)}, bf16[2,128,512]{2,1,0:T(8,128)(2,1)}, u32[]{:S(2)}, u32[]{:S(2)}) collective-permute-start(bf16[2,128,512]{2,1,0:T(8,128)(2,1)S(1)} %get-tuple-element.47), channel_id=1, source_target_pairs={{0,2},{1,3},{2,0},{3,1},{4,6},{5,7},{6,4},{7,5},{8,10},{9,11},{10,... | collective-permute-start | bytes 786440 | tf_op jit(solution)/shard_map/ppermute | solution.py:440
  22.1 0.0 collective-permute-done.11.refs_2_
  22.2 0.6 collective-permute-start.2
  22.7 0.0 collective-permute-done.12.refs_3_
  22.7 3.1 %collective-permute-start.6 = (bf16[512,256]{1,0:T(8,128)(2,1)S(1)}, bf16[512,256]{1,0:T(8,128)(2,1)}, u32[]{:S(2)}, u32[]{:S(2)}) collective-permute-start(bf16[512,256]{1,0:T(8,128)(2,1)S(1)} %get-tuple-element.53.refs_4_), channel_id=1, source_target_pairs={{0,4},{4,8},{8,12},{12,16},{16,20},{20,24},{24,28},{1,5},{5,9},{9,... | collective-permute-start | bytes 786440 | tf_op jit(solution)/shard_map/ppermute | solution.py:461
  25.8 0.0 all-to-all-done.refs_6_
  25.8 0.0 collective-permute-done.13.refs_5_
  25.8 0.0 copy-start.1
  25.9 0.9 %copy-done.1 = bf16[512,256]{1,0:T(8,128)(2,1)S(1)} copy-done((bf16[512,256]{1,0:T(8,128)(2,1)S(1)}, bf16[512,256]{1,0:T(8,128)(2,1)}, u32[]{:S(2)}) %copy-start.1) | copy-done | bytes 262168
  26.8 8.5 %attend.3 = (bf16[2,128,512]{2,1,0:T(8,128)(2,1)S(1)}, bf16[2,128,512]{2,1,0:T(8,128)(2,1)S(1)}, bf16[2,128,512]{2,1,0:T(8,128)(2,1)S(1)}, bf16[2,128,512]{2,1,0...) custom-call(bf16[2,128,512]{2,1,0:T(8,128)(2,1)S(1)} %get-tuple-element.59.refs, ...), custom_call_target="tpu_custom_call" | custom-call | flops 3221225472 | bytes 2097152 | tf_op jit(solution)/shard_map/attend/pallas_call | solution.py:294
  35.3 3.1 %collective-permute-start.21 = (bf16[512,256]{1,0:T(8,128)(2,1)S(1)}, bf16[512,256]{1,0:T(8,128)(2,1)S(1)}, u32[]{:S(2)}, u32[]{:S(2)}) collective-permute-start(bf16[512,256]{1,0:T(8,128)(2,1)S(1)} %get-tuple-element.77), channel_id=1, source_target_pairs={{4,0},{8,4},{12,8},{16,12},{20,16},{24,20},{28,24},{5,1},{9,5},{13... | collective-permute-start | bytes 786440 | tf_op jit(solution)/shard_map/ppermute | solution.py:468
  38.4 0.0 collective-permute-done.refs_1_
  38.4 0.0 collective-permute-done.1.refs_2_
  38.4 0.0 collective-permute-done.2.refs_3_
  38.4 0.0 collective-permute-done.6.refs_5_
  38.4 9.3 %attend.2 = (bf16[2,128,512]{2,1,0:T(8,128)(2,1)S(1)}, bf16[2,128,512]{2,1,0:T(8,128)(2,1)}, bf16[2,128,512]{2,1,0:T(8,128)(2,1)}, bf16[2,128,512]{2,1,0:T(8,128...) custom-call(bf16[2,128,512]{2,1,0:T(8,128)(2,1)S(1)} %get-tuple-element.45.refs_0_, ...), custom_call_target="tpu_custom_call" | custom-call | flops 3221225472 | bytes 2097152 | tf_op jit(solution)/shard_map/attend/pallas_call | solution.py:294
  47.7 2.9 %collective-permute-start.17 = (bf16[512,256]{1,0:T(8,128)(2,1)S(1)}, bf16[512,256]{1,0:T(8,128)(2,1)S(1)}, u32[]{:S(2)}, u32[]{:S(2)}) collective-permute-start(bf16[512,256]{1,0:T(8,128)(2,1)S(1)} %get-tuple-element.71), channel_id=1, source_target_pairs={{4,0},{8,4},{12,8},{16,12},{20,16},{24,20},{28,24},{5,1},{9,5},{13... | collective-permute-start | bytes 786440 | tf_op jit(solution)/shard_map/ppermute | solution.py:466
  50.6 1.1 %collective-permute-start.14 = (bf16[2,128,512]{2,1,0:T(8,128)(2,1)S(1)}, bf16[2,128,512]{2,1,0:T(8,128)(2,1)S(1)}, u32[]{:S(2)}, u32[]{:S(2)}) collective-permute-start(bf16[2,128,512]{2,1,0:T(8,128)(2,1)S(1)} %get-tuple-element.65), channel_id=1, source_target_pairs={{0,1},{1,0},{2,3},{3,2},{4,5},{5,4},{6,7},{7,6},{8,9},{9,8},{10,11... | collective-permute-start | bytes 786440 | tf_op jit(solution)/shard_map/ppermute | solution.py:440
  51.7 1.3 %collective-permute-start.15 = (bf16[2,128,512]{2,1,0:T(8,128)(2,1)S(1)}, bf16[2,128,512]{2,1,0:T(8,128)(2,1)S(1)}, u32[]{:S(2)}, u32[]{:S(2)}) collective-permute-start(bf16[2,128,512]{2,1,0:T(8,128)(2,1)S(1)} %get-tuple-element.66), channel_id=1, source_target_pairs={{0,2},{1,3},{2,0},{3,1},{4,6},{5,7},{6,4},{7,5},{8,10},{9,11},{10,... | collective-permute-start | bytes 786440 | tf_op jit(solution)/shard_map/ppermute | solution.py:440
  53.0 0.4 collective-permute-start.16
  53.4 0.0 collective-permute-done.21.edge
  53.4 0.2 collective-permute-start.7
  53.6 3.1 %collective-permute-done.17.edge = bf16[512,256]{1,0:T(8,128)(2,1)S(1)} collective-permute-done((bf16[512,256]{1,0:T(8,128)(2,1)S(1)}, bf16[512,256]{1,0:T(8,128)(2,1)S(1)}, u32[]{:S(2)}, u32[]{:S(2)}) %collective-permute-start.17) | collective-permute-done | bytes 262176 | tf_op jit(solution)/shard_map/ppermute | solution.py:466
  56.7 1.4 %collective-permute-start.8 = (bf16[2,128,512]{2,1,0:T(8,128)(2,1)}, bf16[2,128,512]{2,1,0:T(8,128)(2,1)S(1)}, u32[]{:S(2)}, u32[]{:S(2)}) collective-permute-start(bf16[2,128,512]{2,1,0:T(8,128)(2,1)} %get-tuple-element.57), channel_id=1, source_target_pairs={{0,2},{1,3},{2,0},{3,1},{4,6},{5,7},{6,4},{7,5},{8,10},{9,11},{10,... | collective-permute-start | bytes 786440 | tf_op jit(solution)/shard_map/ppermute | solution.py:440
  58.1 1.8 %collective-permute-start.9 = (bf16[2,128,512]{2,1,0:T(8,128)(2,1)S(1)}, bf16[2,128,512]{2,1,0:T(8,128)(2,1)S(1)}, u32[]{:S(2)}, u32[]{:S(2)}) collective-permute-start(bf16[2,128,512]{2,1,0:T(8,128)(2,1)S(1)} %get-tuple-element.58), channel_id=1, source_target_pairs={{0,3},{1,2},{2,1},{3,0},{4,7},{5,6},{6,5},{7,4},{8,11},{9,10},{10,... | collective-permute-start | bytes 786440 | tf_op jit(solution)/shard_map/ppermute | solution.py:440
  59.9 0.6 join.3
  60.6 0.0 collective-permute-done.15.refs_6_
  60.6 0.4 collective-permute-start.22
  61.0 0.7 spread.1
  61.6 4.8 %all-to-all-start.1 = ((f32[32,1,512]{2,1,0:T(1,128)}), f32[32,1,512]{2,1,0:T(1,128)S(1)}, u32[]{:S(2)}, u32[]{:S(2)}) async-start(f32[32,1,512]{2,1,0:T(1,128)} %spread.1), calls=%async_computation.1 | async-start | bytes 131072 | tf_op jit(solution)/shard_map/all_to_all | solution.py:471
  66.5 0.7 join.2
  67.2 1.2 %collective-permute-start.23 = (bf16[128,256]{1,0:T(8,128)(2,1)S(1)}, bf16[128,256]{1,0:T(8,128)(2,1)S(1)}, u32[]{:S(2)}, u32[]{:S(2)}) collective-permute-start(bf16[128,256]{1,0:T(8,128)(2,1)S(1)} %get-tuple-element.80), channel_id=1, source_target_pairs={{0,2},{1,3},{2,0},{3,1},{4,6},{5,7},{6,4},{7,5},{8,10},{9,11},{10,... | collective-permute-start | bytes 196616 | tf_op jit(solution)/shard_map/ppermute | solution.py:440
  68.4 0.8 collective-permute-start.24
  69.2 1.9 %collective-permute-done.8.refs_2_ = bf16[2,128,512]{2,1,0:T(8,128)(2,1)S(1)} collective-permute-done((bf16[2,128,512]{2,1,0:T(8,128)(2,1)}, bf16[2,128,512]{2,1,0:T(8,128)(2,1)S(1)}, u32[]{:S(2)}, u32[]{:S(2)}) %collective-permute-start.8) | collective-permute-done | bytes 262176 | tf_op jit(solution)/shard_map/ppermute | solution.py:440
  71.1 1.6 %collective-permute-start.18 = (bf16[128,256]{1,0:T(8,128)(2,1)}, bf16[128,256]{1,0:T(8,128)(2,1)S(1)}, u32[]{:S(2)}, u32[]{:S(2)}) collective-permute-start(bf16[128,256]{1,0:T(8,128)(2,1)} %get-tuple-element.73), channel_id=1, source_target_pairs={{0,1},{1,0},{2,3},{3,2},{4,5},{5,4},{6,7},{7,6},{8,9},{9,8},{10,11... | collective-permute-start | bytes 196616 | tf_op jit(solution)/shard_map/ppermute | solution.py:440
  72.7 5.2 %collective-permute-done.9.refs_3_ = bf16[2,128,512]{2,1,0:T(8,128)(2,1)S(1)} collective-permute-done((bf16[2,128,512]{2,1,0:T(8,128)(2,1)S(1)}, bf16[2,128,512]{2,1,0:T(8,128)(2,1)S(1)}, u32[]{:S(2)}, u32[]{:S(2)}) %collective-permute-start.9) | collective-permute-done | bytes 262176 | tf_op jit(solution)/shard_map/ppermute | solution.py:440
  78.0 1.3 %collective-permute-start.19 = (bf16[128,256]{1,0:T(8,128)(2,1)}, bf16[128,256]{1,0:T(8,128)(2,1)S(1)}, u32[]{:S(2)}, u32[]{:S(2)}) collective-permute-start(bf16[128,256]{1,0:T(8,128)(2,1)} %get-tuple-element.74), channel_id=1, source_target_pairs={{0,2},{1,3},{2,0},{3,1},{4,6},{5,7},{6,4},{7,5},{8,10},{9,11},{10,... | collective-permute-start | bytes 196616 | tf_op jit(solution)/shard_map/ppermute | solution.py:440
  79.3 0.0 collective-permute-done.22.refs_5_
  79.3 0.0 collective-permute-start.20
  79.3 1.4 %unpack.1 = (bf16[128,4096]{1,0:T(8,128)(2,1)}, bf16[128,4096]{1,0:T(8,128)(2,1)}) custom-call(bf16[2,128,512]{2,1,0:T(8,128)(2,1)S(1)} %get-tuple-element.55.refs_0_, bf16[2,128,512]{2,1,0:T(8,128)(2,1)S(1)} %collective-permute-done.7.refs_1_, bf16[2,128,512]{2,1,0:T(8,128)(2,1)S(1)} %collective-permute-done.8.refs_2_, ...), custom_call_target="tpu_custom_call" | custom-call | tf_op jit(solution)/shard_map/unpack/pallas_call | solution.py:392
  80.7 0.0 all-to-all-done.1.refs_8_
  80.7 0.0 collective-permute-done.24.refs_7_
  80.8 0.0 collective-permute-done.18.refs_1_
  80.8 1.4 %collective-permute-done.19.refs_2_ = bf16[128,256]{1,0:T(8,128)(2,1)S(1)} collective-permute-done((bf16[128,256]{1,0:T(8,128)(2,1)}, bf16[128,256]{1,0:T(8,128)(2,1)S(1)}, u32[]{:S(2)}, u32[]{:S(2)}) %collective-permute-start.19) | collective-permute-done | bytes 65568 | tf_op jit(solution)/shard_map/ppermute | solution.py:440
  82.2 1.1 %collective-permute-done.20.refs_3_ = bf16[128,256]{1,0:T(8,128)(2,1)S(1)} collective-permute-done((bf16[128,256]{1,0:T(8,128)(2,1)}, bf16[128,256]{1,0:T(8,128)(2,1)S(1)}, u32[]{:S(2)}, u32[]{:S(2)}) %collective-permute-start.20) | collective-permute-done | bytes 65568 | tf_op jit(solution)/shard_map/ppermute | solution.py:440
  83.4 1.0 %finish.1 = (bf16[128,1024]{1,0:T(8,128)(2,1)}, bf16[128,1024]{1,0:T(8,128)(2,1)}) custom-call(bf16[128,256]{1,0:T(8,128)(2,1)S(1)} %get-tuple-element.72.refs_0_, bf16[128,256]{1,0:T(8,128)(2,1)S(1)} %collective-permute-done.18.refs_1_, bf16[128,256]{1,0:T(8,128)(2,1)S(1)} %collective-permute-done.19.refs_2_, ...), custom_call_target="tpu_custom_call" | custom-call | tf_op jit(solution)/shard_map/finish/pallas_call | solution.py:424
  (4 shorter events, 0.0 us)
Async XLA Ops:
  1.8 6.4 %collective-permute-start.3 = (bf16[128,512]{1,0:T(8,128)(2,1)S(1)}, bf16[128,512]{1,0:T(8,128)(2,1)S(1)}, u32[]{:S(2)}, u32[]{:S(2)}) collective-permute-start(bf16[128,512]{1,0:T(8,128)(2,1)S(1)} %get-tuple-element.50), channel_id=1, source_target_pairs={{0,1},{1,0},{2,3},{3,2},{4,5},{5,4},{6,7},{7,6},{8,9},{9,8},{10,11... | collective-permute-start | bytes 393224 | tf_op jit(solution)/shard_map/ppermute | solution.py:440
  2.5 6.5 %collective-permute-start.4 = (bf16[128,512]{1,0:T(8,128)(2,1)S(1)}, bf16[128,512]{1,0:T(8,128)(2,1)S(1)}, u32[]{:S(2)}, u32[]{:S(2)}) collective-permute-start(bf16[128,512]{1,0:T(8,128)(2,1)S(1)} %get-tuple-element.51), channel_id=1, source_target_pairs={{0,2},{1,3},{2,0},{3,1},{4,6},{5,7},{6,4},{7,5},{8,10},{9,11},{10,... | collective-permute-start | bytes 393224 | tf_op jit(solution)/shard_map/ppermute | solution.py:440
  3.7 7.4 %collective-permute-start.5 = (bf16[128,512]{1,0:T(8,128)(2,1)S(1)}, bf16[128,512]{1,0:T(8,128)(2,1)S(1)}, u32[]{:S(2)}, u32[]{:S(2)}) collective-permute-start(bf16[128,512]{1,0:T(8,128)(2,1)S(1)} %get-tuple-element.52), channel_id=1, source_target_pairs={{0,3},{1,2},{2,1},{3,0},{4,7},{5,6},{6,5},{7,4},{8,11},{9,10},{10,... | collective-permute-start | bytes 393224 | tf_op jit(solution)/shard_map/ppermute | solution.py:440
  6.8 14.2 %collective-permute-start.10 = (bf16[2,128,512]{2,1,0:T(8,128)(2,1)}, bf16[2,128,512]{2,1,0:T(8,128)(2,1)S(1)}, u32[]{:S(2)}, u32[]{:S(2)}) collective-permute-start(bf16[2,128,512]{2,1,0:T(8,128)(2,1)} %get-tuple-element.60), channel_id=1, source_target_pairs={{0,1},{1,0},{2,3},{3,2},{4,5},{5,4},{6,7},{7,6},{8,9},{9,8},{10,11... | collective-permute-start | bytes 786440 | tf_op jit(solution)/shard_map/ppermute | solution.py:440
  7.0 15.2 %collective-permute-start.11 = (bf16[2,128,512]{2,1,0:T(8,128)(2,1)}, bf16[2,128,512]{2,1,0:T(8,128)(2,1)S(1)}, u32[]{:S(2)}, u32[]{:S(2)}) collective-permute-start(bf16[2,128,512]{2,1,0:T(8,128)(2,1)} %get-tuple-element.61), channel_id=1, source_target_pairs={{0,2},{1,3},{2,0},{3,1},{4,6},{5,7},{6,4},{7,5},{8,10},{9,11},{10,... | collective-permute-start | bytes 786440 | tf_op jit(solution)/shard_map/ppermute | solution.py:440
  8.2 14.5 %collective-permute-start.12 = (bf16[2,128,512]{2,1,0:T(8,128)(2,1)S(1)}, bf16[2,128,512]{2,1,0:T(8,128)(2,1)S(1)}, u32[]{:S(2)}, u32[]{:S(2)}) collective-permute-start(bf16[2,128,512]{2,1,0:T(8,128)(2,1)S(1)} %get-tuple-element.62), channel_id=1, source_target_pairs={{0,3},{1,2},{2,1},{3,0},{4,7},{5,6},{6,5},{7,4},{8,11},{9,10},{10,... | collective-permute-start | bytes 786440 | tf_op jit(solution)/shard_map/ppermute | solution.py:440
  11.9 14.0 %collective-permute-start.13 = (bf16[512,256]{1,0:T(8,128)(2,1)S(1)}, bf16[512,256]{1,0:T(8,128)(2,1)}, u32[]{:S(2)}, u32[]{:S(2)}) collective-permute-start(bf16[512,256]{1,0:T(8,128)(2,1)S(1)} %get-tuple-element.63.refs_4_), channel_id=1, source_target_pairs={{0,4},{4,8},{8,12},{12,16},{16,20},{20,24},{24,28},{1,5},{5,9},{9,... | collective-permute-start | bytes 786440 | tf_op jit(solution)/shard_map/ppermute | solution.py:462
  15.0 0.7 copy-start
  15.7 10.1 %all-to-all-start = ((f32[8,1,512]{2,1,0:T(1,128)}), f32[8,1,512]{2,1,0:T(1,128)S(1)}, u32[]{:S(2)}, u32[]{:S(2)}) async-start(f32[8,1,512]{2,1,0:T(1,128)} %get-tuple-element.54), calls=%async_computation | async-start | bytes 32768 | tf_op jit(solution)/shard_map/all_to_all | solution.py:463
  20.5 17.9 %collective-permute-start = (bf16[2,128,512]{2,1,0:T(8,128)(2,1)S(1)}, bf16[2,128,512]{2,1,0:T(8,128)(2,1)S(1)}, u32[]{:S(2)}, u32[]{:S(2)}) collective-permute-start(bf16[2,128,512]{2,1,0:T(8,128)(2,1)S(1)} %get-tuple-element.46), channel_id=1, source_target_pairs={{0,1},{1,0},{2,3},{3,2},{4,5},{5,4},{6,7},{7,6},{8,9},{9,8},{10,11... | collective-permute-start | bytes 786440 | tf_op jit(solution)/shard_map/ppermute | solution.py:440
  21.0 17.4 %collective-permute-start.1 = (bf16[2,128,512]{2,1,0:T(8,128)(2,1)S(1)}, bf16[2,128,512]{2,1,0:T(8,128)(2,1)}, u32[]{:S(2)}, u32[]{:S(2)}) collective-permute-start(bf16[2,128,512]{2,1,0:T(8,128)(2,1)S(1)} %get-tuple-element.47), channel_id=1, source_target_pairs={{0,2},{1,3},{2,0},{3,1},{4,6},{5,7},{6,4},{7,5},{8,10},{9,11},{10,... | collective-permute-start | bytes 786440 | tf_op jit(solution)/shard_map/ppermute | solution.py:440
  22.2 16.2 %collective-permute-start.2 = (bf16[2,128,512]{2,1,0:T(8,128)(2,1)S(1)}, bf16[2,128,512]{2,1,0:T(8,128)(2,1)}, u32[]{:S(2)}, u32[]{:S(2)}) collective-permute-start(bf16[2,128,512]{2,1,0:T(8,128)(2,1)S(1)} %get-tuple-element.48), channel_id=1, source_target_pairs={{0,3},{1,2},{2,1},{3,0},{4,7},{5,6},{6,5},{7,4},{8,11},{9,10},{10,... | collective-permute-start | bytes 786440 | tf_op jit(solution)/shard_map/ppermute | solution.py:440
  22.7 15.7 %collective-permute-start.6 = (bf16[512,256]{1,0:T(8,128)(2,1)S(1)}, bf16[512,256]{1,0:T(8,128)(2,1)}, u32[]{:S(2)}, u32[]{:S(2)}) collective-permute-start(bf16[512,256]{1,0:T(8,128)(2,1)S(1)} %get-tuple-element.53.refs_4_), channel_id=1, source_target_pairs={{0,4},{4,8},{8,12},{12,16},{16,20},{20,24},{24,28},{1,5},{5,9},{9,... | collective-permute-start | bytes 786440 | tf_op jit(solution)/shard_map/ppermute | solution.py:461
  25.8 1.0 %copy-start.1 = (bf16[512,256]{1,0:T(8,128)(2,1)S(1)}, bf16[512,256]{1,0:T(8,128)(2,1)}, u32[]{:S(2)}) copy-start(bf16[512,256]{1,0:T(8,128)(2,1)} %copy-done) | copy-start | bytes 786436
  35.3 18.2 %collective-permute-start.21 = (bf16[512,256]{1,0:T(8,128)(2,1)S(1)}, bf16[512,256]{1,0:T(8,128)(2,1)S(1)}, u32[]{:S(2)}, u32[]{:S(2)}) collective-permute-start(bf16[512,256]{1,0:T(8,128)(2,1)S(1)} %get-tuple-element.77), channel_id=1, source_target_pairs={{4,0},{8,4},{12,8},{16,12},{20,16},{24,20},{28,24},{5,1},{9,5},{13... | collective-permute-start | bytes 786440 | tf_op jit(solution)/shard_map/ppermute | solution.py:468
  47.7 9.0 %collective-permute-start.17 = (bf16[512,256]{1,0:T(8,128)(2,1)S(1)}, bf16[512,256]{1,0:T(8,128)(2,1)S(1)}, u32[]{:S(2)}, u32[]{:S(2)}) collective-permute-start(bf16[512,256]{1,0:T(8,128)(2,1)S(1)} %get-tuple-element.71), channel_id=1, source_target_pairs={{4,0},{8,4},{12,8},{16,12},{20,16},{24,20},{28,24},{5,1},{9,5},{13... | collective-permute-start | bytes 786440 | tf_op jit(solution)/shard_map/ppermute | solution.py:466
  50.6 7.5 %collective-permute-start.14 = (bf16[2,128,512]{2,1,0:T(8,128)(2,1)S(1)}, bf16[2,128,512]{2,1,0:T(8,128)(2,1)S(1)}, u32[]{:S(2)}, u32[]{:S(2)}) collective-permute-start(bf16[2,128,512]{2,1,0:T(8,128)(2,1)S(1)} %get-tuple-element.65), channel_id=1, source_target_pairs={{0,1},{1,0},{2,3},{3,2},{4,5},{5,4},{6,7},{7,6},{8,9},{9,8},{10,11... | collective-permute-start | bytes 786440 | tf_op jit(solution)/shard_map/ppermute | solution.py:440
  51.7 8.9 %collective-permute-start.15 = (bf16[2,128,512]{2,1,0:T(8,128)(2,1)S(1)}, bf16[2,128,512]{2,1,0:T(8,128)(2,1)S(1)}, u32[]{:S(2)}, u32[]{:S(2)}) collective-permute-start(bf16[2,128,512]{2,1,0:T(8,128)(2,1)S(1)} %get-tuple-element.66), channel_id=1, source_target_pairs={{0,2},{1,3},{2,0},{3,1},{4,6},{5,7},{6,4},{7,5},{8,10},{9,11},{10,... | collective-permute-start | bytes 786440 | tf_op jit(solution)/shard_map/ppermute | solution.py:440
  53.0 14.1 %collective-permute-start.16 = (bf16[2,128,512]{2,1,0:T(8,128)(2,1)S(1)}, bf16[2,128,512]{2,1,0:T(8,128)(2,1)S(1)}, u32[]{:S(2)}, u32[]{:S(2)}) collective-permute-start(bf16[2,128,512]{2,1,0:T(8,128)(2,1)S(1)} %get-tuple-element.67), channel_id=1, source_target_pairs={{0,3},{1,2},{2,1},{3,0},{4,7},{5,6},{6,5},{7,4},{8,11},{9,10},{10,... | collective-permute-start | bytes 786440 | tf_op jit(solution)/shard_map/ppermute | solution.py:440
  53.4 14.9 %collective-permute-start.7 = (bf16[2,128,512]{2,1,0:T(8,128)(2,1)}, bf16[2,128,512]{2,1,0:T(8,128)(2,1)S(1)}, u32[]{:S(2)}, u32[]{:S(2)}) collective-permute-start(bf16[2,128,512]{2,1,0:T(8,128)(2,1)} %get-tuple-element.56), channel_id=1, source_target_pairs={{0,1},{1,0},{2,3},{3,2},{4,5},{5,4},{6,7},{7,6},{8,9},{9,8},{10,11... | collective-permute-start | bytes 786440 | tf_op jit(solution)/shard_map/ppermute | solution.py:440
  56.7 14.4 %collective-permute-start.8 = (bf16[2,128,512]{2,1,0:T(8,128)(2,1)}, bf16[2,128,512]{2,1,0:T(8,128)(2,1)S(1)}, u32[]{:S(2)}, u32[]{:S(2)}) collective-permute-start(bf16[2,128,512]{2,1,0:T(8,128)(2,1)} %get-tuple-element.57), channel_id=1, source_target_pairs={{0,2},{1,3},{2,0},{3,1},{4,6},{5,7},{6,4},{7,5},{8,10},{9,11},{10,... | collective-permute-start | bytes 786440 | tf_op jit(solution)/shard_map/ppermute | solution.py:440
  58.1 19.9 %collective-permute-start.9 = (bf16[2,128,512]{2,1,0:T(8,128)(2,1)S(1)}, bf16[2,128,512]{2,1,0:T(8,128)(2,1)S(1)}, u32[]{:S(2)}, u32[]{:S(2)}) collective-permute-start(bf16[2,128,512]{2,1,0:T(8,128)(2,1)S(1)} %get-tuple-element.58), channel_id=1, source_target_pairs={{0,3},{1,2},{2,1},{3,0},{4,7},{5,6},{6,5},{7,4},{8,11},{9,10},{10,... | collective-permute-start | bytes 786440 | tf_op jit(solution)/shard_map/ppermute | solution.py:440
  60.6 18.7 %collective-permute-start.22 = (bf16[128,256]{1,0:T(8,128)(2,1)}, bf16[128,256]{1,0:T(8,128)(2,1)S(1)}, u32[]{:S(2)}, u32[]{:S(2)}) collective-permute-start(bf16[128,256]{1,0:T(8,128)(2,1)} %get-tuple-element.79), channel_id=1, source_target_pairs={{0,1},{1,0},{2,3},{3,2},{4,5},{5,4},{6,7},{7,6},{8,9},{9,8},{10,11... | collective-permute-start | bytes 196616 | tf_op jit(solution)/shard_map/ppermute | solution.py:440
  61.6 19.1 %all-to-all-start.1 = ((f32[32,1,512]{2,1,0:T(1,128)}), f32[32,1,512]{2,1,0:T(1,128)S(1)}, u32[]{:S(2)}, u32[]{:S(2)}) async-start(f32[32,1,512]{2,1,0:T(1,128)} %spread.1), calls=%async_computation.1 | async-start | bytes 131072 | tf_op jit(solution)/shard_map/all_to_all | solution.py:471
  67.2 13.6 %collective-permute-start.23 = (bf16[128,256]{1,0:T(8,128)(2,1)S(1)}, bf16[128,256]{1,0:T(8,128)(2,1)S(1)}, u32[]{:S(2)}, u32[]{:S(2)}) collective-permute-start(bf16[128,256]{1,0:T(8,128)(2,1)S(1)} %get-tuple-element.80), channel_id=1, source_target_pairs={{0,2},{1,3},{2,0},{3,1},{4,6},{5,7},{6,4},{7,5},{8,10},{9,11},{10,... | collective-permute-start | bytes 196616 | tf_op jit(solution)/shard_map/ppermute | solution.py:440
  68.4 12.4 %collective-permute-start.24 = (bf16[128,256]{1,0:T(8,128)(2,1)S(1)}, bf16[128,256]{1,0:T(8,128)(2,1)S(1)}, u32[]{:S(2)}, u32[]{:S(2)}) collective-permute-start(bf16[128,256]{1,0:T(8,128)(2,1)S(1)} %get-tuple-element.81), channel_id=1, source_target_pairs={{0,3},{1,2},{2,1},{3,0},{4,7},{5,6},{6,5},{7,4},{8,11},{9,10},{10,... | collective-permute-start | bytes 196616 | tf_op jit(solution)/shard_map/ppermute | solution.py:440
  71.1 9.6 %collective-permute-start.18 = (bf16[128,256]{1,0:T(8,128)(2,1)}, bf16[128,256]{1,0:T(8,128)(2,1)S(1)}, u32[]{:S(2)}, u32[]{:S(2)}) collective-permute-start(bf16[128,256]{1,0:T(8,128)(2,1)} %get-tuple-element.73), channel_id=1, source_target_pairs={{0,1},{1,0},{2,3},{3,2},{4,5},{5,4},{6,7},{7,6},{8,9},{9,8},{10,11... | collective-permute-start | bytes 196616 | tf_op jit(solution)/shard_map/ppermute | solution.py:440
  78.0 4.2 %collective-permute-start.19 = (bf16[128,256]{1,0:T(8,128)(2,1)}, bf16[128,256]{1,0:T(8,128)(2,1)S(1)}, u32[]{:S(2)}, u32[]{:S(2)}) collective-permute-start(bf16[128,256]{1,0:T(8,128)(2,1)} %get-tuple-element.74), channel_id=1, source_target_pairs={{0,2},{1,3},{2,0},{3,1},{4,6},{5,7},{6,4},{7,5},{8,10},{9,11},{10,... | collective-permute-start | bytes 196616 | tf_op jit(solution)/shard_map/ppermute | solution.py:440
  79.3 4.1 %collective-permute-start.20 = (bf16[128,256]{1,0:T(8,128)(2,1)}, bf16[128,256]{1,0:T(8,128)(2,1)S(1)}, u32[]{:S(2)}, u32[]{:S(2)}) collective-permute-start(bf16[128,256]{1,0:T(8,128)(2,1)} %get-tuple-element.75), channel_id=1, source_target_pairs={{0,3},{1,2},{2,1},{3,0},{4,7},{5,6},{6,5},{7,4},{8,11},{9,10},{10,... | collective-permute-start | bytes 196616 | tf_op jit(solution)/shard_map/ppermute | solution.py:440
